TPU v7x, 1024 devices: a whole 8x8x8 slice. The times are simulated.
1024 devices in a mesh: seq: 32 (over x, z_hi), head: 32 (over y, z_lo, core).
Axes of the slice: x: 8, y: 8, z: 8 (z_hi: 4, z_lo: 2; z = z_hi * 2 + z_lo), core: 2. Of those that a mesh axis runs over, the one named last changes fastest.
Arguments:
- inputs: bfloat16 [24576, 8192], P('seq', 'head'), may hold values from -6 to 6
- log_decay: float32 [128, 24576], P('head', 'seq'), may hold values from -3 to 0, as said below
- write_proj: bfloat16 [24576, 128], P('seq'), may hold values from -0.5 to 0.5
- read_proj: bfloat16 [24576, 128], P('seq'), may hold values from -0.5 to 0.5
- grad_out: bfloat16 [24576, 8192], P('seq', 'head'), may hold values from -0.75 to 0.75
Outputs:
- outputs: bfloat16 [24576, 8192], P('seq', 'head')
- grad_inputs: bfloat16 [24576, 8192], P('seq', 'head')
- grad_write: float32 [24576, 128], P(('seq', 'head'))
- grad_read: float32 [24576, 128], P(('seq', 'head'))
Inputs may be any that keep to these rules, and one draw needn't show every extreme that they name: log_decay is negative everywhere.
All inputs are finite; a program needn't handle non-finite values.
Results may differ from a plain program's by a relative error of at most 0.0032.
Values sent between devices are 32-bit elements; how exact they have to be, the bound alone decides.
No kernel may reach another device: no remote copies, remote signals or barrier semaphores. Data moves between devices by JAX's collectives and lax.ppermute only.
A program may use at most 64 MiB of HBM per device.

v0:
```python
import jax
import jax.numpy as jnp
from jax import lax
from jax.sharding import PartitionSpec as P

highest = lax.Precision.HIGHEST


def carried_in(value, axis, join, neutral, backward):
    count, mine = (lax.axis_size(axis), lax.axis_index(axis))
    pieces = jax.tree.map(lambda part: lax.all_gather(part, axis), value)
    if backward:
        pieces = jax.tree.map(lambda part: part[::-1], pieces)
        mine = count - 1 - mine
    running = jax.tree.map(
        lambda part, zero: jnp.full_like(part, 0) + jnp.asarray(zero, part.dtype), value, neutral
    )

    def lap(position, running):
        longer = join(running, jax.tree.map(lambda part: part[position], pieces))
        return jax.tree.map(lambda new, old: jnp.where(position < mine, new, old), longer, running)

    return lax.fori_loop(0, count - 1, lap, running)


def combine(earlier, later):
    return (earlier[0] * later[0], later[0][:, None, None] * earlier[1] + later[1])


def per_device(inputs, log_decay, write_proj, read_proj, grad_out):
    tok_rows = inputs.shape[0]
    heads_here = log_decay.shape[0]
    head_size = inputs.shape[1] // heads_here
    state_size = write_proj.shape[1]
    cumulative = jnp.cumsum(log_decay, axis=1)
    last_cumul = cumulative[:, -1:]
    tail_weight = jnp.exp(last_cumul - cumulative)
    lead_weight = jnp.exp(cumulative)
    decay_total = jnp.exp(last_cumul[:, 0])
    x_heads = inputs.reshape(tok_rows, heads_here, head_size)
    g_heads = grad_out.reshape(tok_rows, heads_here, head_size)
    x_wide = x_heads.astype(jnp.float32)
    g_wide = g_heads.astype(jnp.float32)
    write_wide = write_proj.astype(jnp.float32)
    read_wide = read_proj.astype(jnp.float32)
    local_state = jnp.einsum(
        "jhp,jn->hpn", x_wide * tail_weight.T[:, :, None], write_wide, precision=highest
    )
    local_grad = jnp.einsum(
        "thp,tn->hpn", g_wide * lead_weight.T[:, :, None], read_wide, precision=highest
    )
    identity = (jnp.ones_like(decay_total), jnp.zeros_like(local_state))
    _, state_in = carried_in((decay_total, local_state), "seq", combine, identity, False)
    _, grad_state = carried_in((decay_total, local_grad), "seq", combine, identity, True)
    rows_index = lax.broadcasted_iota(jnp.int32, (tok_rows, tok_rows), 0)
    cols_index = lax.broadcasted_iota(jnp.int32, (tok_rows, tok_rows), 1)
    causal = rows_index >= cols_index
    scores = jnp.dot(read_proj, write_proj.T, preferred_element_type=jnp.float32)
    grad_score = jnp.zeros((tok_rows, tok_rows), jnp.float32)
    y_parts = []
    dx_parts = []
    for head_pos in range(heads_here):
        differ = cumulative[head_pos][:, None] - cumulative[head_pos][None, :]
        decay_mat = jnp.exp(jnp.where(causal, differ, -jnp.inf))
        mixing = (scores * decay_mat).astype(jnp.bfloat16)
        x_head = x_heads[:, head_pos, :]
        g_head = g_heads[:, head_pos, :]
        y_parts.append(jnp.dot(mixing, x_head, preferred_element_type=jnp.float32))
        dx_parts.append(jnp.einsum("tj,tp->jp", mixing, g_head, preferred_element_type=jnp.float32))
        grad_prod = jnp.einsum("tp,jp->tj", g_head, x_head, preferred_element_type=jnp.float32)
        grad_score = grad_score + grad_prod * decay_mat
    y_intra = jnp.stack(y_parts, axis=1)
    dx_intra = jnp.stack(dx_parts, axis=1)
    y_inter = (
        jnp.einsum("tn,hpn->thp", read_wide, state_in, precision=highest)
        * lead_weight.T[:, :, None]
    )
    outputs = (y_intra + y_inter).astype(jnp.bfloat16).reshape(tok_rows, heads_here * head_size)
    dx_inter = (
        jnp.einsum("jn,hpn->jhp", write_wide, grad_state, precision=highest)
        * tail_weight.T[:, :, None]
    )
    grad_inputs = (
        (dx_intra + dx_inter).astype(jnp.bfloat16).reshape(tok_rows, heads_here * head_size)
    )
    grad_write = jnp.dot(grad_score.T, read_wide, precision=highest) + jnp.einsum(
        "jhp,hpn->jn", x_wide * tail_weight.T[:, :, None], grad_state, precision=highest
    )
    grad_read = jnp.dot(grad_score, write_wide, precision=highest) + jnp.einsum(
        "thp,hpn->tn", g_wide * lead_weight.T[:, :, None], state_in, precision=highest
    )
    grad_pair = jnp.concatenate([grad_write, grad_read], axis=1)
    summed = lax.psum_scatter(grad_pair, "head", scatter_dimension=0, tiled=True)
    return (outputs, grad_inputs, summed[:, :state_size], summed[:, state_size:])


def solution(mesh):
    return jax.shard_map(
        per_device,
        mesh=mesh,
        in_specs=(
            P("seq", "head"),
            P("head", "seq"),
            P("seq", None),
            P("seq", None),
            P("seq", "head"),
        ),
        out_specs=(
            P("seq", "head"),
            P("seq", "head"),
            P(("seq", "head"), None),
            P(("seq", "head"), None),
        ),
        check_vma=False,
    )
```

profile of v0, /device:TPU:12, one launch (start us, length us, event | category | flops | bytes accessed | tf_op | source)
XLA Modules:
  0.0 418.0 jit_solution(12925990136869396204)
XLA Ops:
  11.0 2.1 fusion.9
  15.7 2.0 fusion.20
  17.7 1.9 fusion.19
  19.6 1.9 fusion.18
  23.6 85.4 %all-reduce = f32[128]{0:T(128)S(1)} all-reduce(f32[128]{0:T(128)S(1)} %dynamic-update-slice), channel_id=2, replica_groups=mesh['seq'=32,'head'=32] {'seq'}, use_global_device_ids=true, to_apply=%add | all-reduce | flops 128 | bytes 1024
  109.1 3.6 multiply_convert_fusion.3
  114.8 4.5 %multiply_add_fusion = f32[768,768]{1,0:T(8,128)S(1)} fusion(f32[768,768]{1,0:T(8,128)} %fusion.20, f32[768,768]{1,0:T(8,128)} %fusion.19, f32[768,768]{1,0:T(8,128)} %fusion.18, f32[768]{0:T(1024)S(1)} %get-tuple-element.277, f32[768]{0:T(1024)S(1)} %get-tuple-element.278, f32[768]{0:T(1024)S(1)} %get-tuple-element.279, f32[768]{0:T(1024)S(1)} %get-tuple-element.276, ...), kind=kOutput, calls=%fused_computation.6 | convolution fusion | flops 84934656 | bytes 9666560 | tf_op jit(solution)/shard_map/tp,jp->tj/dot_general | solution.py:70
  119.3 14.8 %all-gather.6.cloned.1.call-done = f32[128,64,128]{2,1,0:T(8,128)} async-done(((f32[4,64,128]{2,1,0:T(8,128)}), f32[128,64,128]{2,1,0:T(8,128)}) %all-gather.6.cloned.1.call-update) | async-done | bytes 4194320 | tf_op jit(solution)/shard_map/all_gather | solution.py:11
  134.0 53.1 %while.28 = (s32[]{:T(128)}, f32[4,64,128]{2,1,0:T(8,128)}, s32[]{:T(128)}, f32[32,4]{1,0:T(8,128)S(1)}, f32[32,4,64,128]{3,2,1,0:T(8,128)}, /*index=5*/s32[]{:T(128)}, s32[]{:T(128)}) while((s32[]{:T(128)}, f32[4,64,128]{2,1,0:T(8,128)}, s32[]{:T(128)}, f32[32,4]{1,0:T(8,128)S(1)}, f32[32,4,64,128]{3,2,1,0:T(8,128)}, ...), condition=%wide.region_3.4_spmd.clone, body=%wide.region_2.3_spmd.clone.sunk | while | flops 131076 | bytes 393377 | solution.py:23
  140.8 1.7 fusion.43
  149.4 1.7 fusion.43
  151.1 1.7 fusion.43
  152.8 1.7 fusion.43
  161.4 1.7 fusion.43
  164.9 1.7 fusion.43
  168.3 1.7 fusion.43
  175.1 1.7 fusion.43
  176.9 1.7 fusion.43
  187.1 57.7 %all-gather.8.cloned.1.call-done = f32[128,64,128]{2,1,0:T(8,128)} async-done(((f32[4,64,128]{2,1,0:T(8,128)}), f32[128,64,128]{2,1,0:T(8,128)}) %all-gather.8.cloned.1.call-update) | async-done | bytes 4194320 | tf_op jit(solution)/shard_map/all_gather | solution.py:11
  244.8 4.8 %rev.7 = f32[32,4,64,128]{3,2,1,0:T(8,128)} reverse(f32[32,4,64,128]{3,2,1,0:T(8,128)} %bitcast.162), dimensions={0} | reverse | bytes 8388608 | tf_op jit(solution)/shard_map/rev | solution.py:13
  249.6 32.3 %while.29 = (s32[]{:T(128)}, f32[4,64,128]{2,1,0:T(8,128)S(1)}, s32[]{:T(128)}, f32[32,4]{1,0:T(8,128)S(1)}, f32[32,4,64,128]{3,2,1,0:T(8,128)}, /*index=5*/s32[]{:T(128)}, s32[]{:T(128)}) while((s32[]{:T(128)}, f32[4,64,128]{2,1,0:T(8,128)S(1)}, s32[]{:T(128)}, f32[32,4]{1,0:T(8,128)S(1)}, f32[32,4,64,128]{3,2,1,0:T(8,128)}, ...), condition=%wide.region_5.6_spmd.clone, body=%wide.region_4.5_spmd.clone.sunk | while | flops 131076 | bytes 393377 | solution.py:23
  284.0 2.3 convolution_add_fusion
  288.3 2.3 copy.34
  296.6 113.6 %reduce-scatter.4.cloned.1.call-done = f32[24,256]{1,0:T(8,128)} async-done(((f32[768,256]{1,0:T(8,128)}), f32[24,256]{1,0:T(8,128)}) %reduce-scatter.4.cloned.1.call-update) | async-done | bytes 24592
  (178 shorter events, 90.2 us)
Async XLA Ops:
  7.2 7.2 %copy-start = (bf16[768,128]{1,0:T(8,128)(2,1)S(1)}, bf16[768,128]{1,0:T(8,128)(2,1)}, u32[]{:S(2)}) copy-start(bf16[768,128]{1,0:T(8,128)(2,1)} %param.12) | copy-start | bytes 589828
  7.2 126.8 %all-gather.6.cloned.1.call-start = ((), (), s32[]{:S(2)}) async-start(), calls=%async_computation.1 | async-start | bytes 4325376 | tf_op jit(solution)/shard_map/all_gather | solution.py:11
  13.1 231.7 %all-gather.8.cloned.1.call-start = ((), (), s32[]{:S(2)}) async-start(), calls=%async_computation.2 | async-start | bytes 4325376 | tf_op jit(solution)/shard_map/all_gather | solution.py:11
  15.6 394.6 %reduce-scatter.4.cloned.1.call-start = ((), (), s32[]{:S(2)}) async-start(), calls=%async_computation.3 | async-start | bytes 811008
  17.7 91.5 %copy-start.7 = (bf16[768,128]{1,0:T(8,128)(2,1)S(1)}, bf16[768,128]{1,0:T(8,128)(2,1)}, u32[]{:S(2)}) copy-start(bf16[768,128]{1,0:T(8,128)(2,1)} %param.11) | copy-start | bytes 589828
  112.7 1.0 copy-start.5
  287.3 3.3 copy-start.6
  287.4 3.8 copy-start.4
  290.7 1.4 copy-start.3
  291.5 1.4 copy-start.2
  292.4 1.4 copy-start.1
  293.4 1.8 copy-start.8
  293.4 1.8 copy-start.9
Sparse Core Ops, SparseCore 0:
  13.2 120.7 all-gather.5
  138.4 106.3 all-gather.7
  290.8 119.3 reduce-scatter.3
where the time goes:
time: 420 us; the launch traced here: 418 us
  waiting for transfers between devices  186 us (44%)
  other arithmetic  86.3 us (21%)
  blocking collectives  85.4 us (20%)
  matrix products  27.5 us (7%)
  local copies, waits for them, and re-layouts  17 us (4%)
  between operations  14.6 us (3%)
    unnamed x4, waiting for transfers between devices  114 us
    unnamed x1, blocking collectives  85.4 us
    select_n x62, other arithmetic, lap(): jnp.where(position < mine, new, old)  83.8 us
    all_gather x2, waiting for transfers between devices, carried_in(): pieces = jax.tree.map(lambda part: lax.all_gather(part, axis), value)  72.4 us
    dot_general x4, matrix products, per_device(): jnp.einsum('tp,jp->tj', g_head, x_head, preferred_element_type=jnp.float32)  10.3 us
    unnamed x28, local copies, waits for them, and re-layouts  9.14 us
  transfers between devices with their start and end apart: 3, of which 3 were waited for; matrix products, arithmetic and copies ran while one was open for 19% of the time, Pallas kernels for 0%

commit v1 on v0

v1 whole, which is shorter than its diff:
```python
import functools

import jax
import jax.numpy as jnp
from jax import lax
from jax.experimental import pallas as pl
from jax.experimental.pallas import tpu as pltpu
from jax.sharding import Mesh, PartitionSpec as P

f32 = jnp.float32
bf16 = jnp.bfloat16
VMEM = pl.BlockSpec(memory_space=pltpu.VMEM)
SMEM = pl.BlockSpec(memory_space=pltpu.SMEM)
BLOCK = 256


def dot(a, b, dims):
    return lax.dot_general(a, b, (dims, ((), ())), preferred_element_type=f32)


def split(value):
    high = value.astype(bf16)
    return high, (value - high.astype(f32)).astype(bf16)


def lanes_of_heads(columns, heads, width):
    tokens = columns.shape[0]
    lane = lax.broadcasted_iota(jnp.int32, (tokens, heads * width), 1) // width
    spread = jnp.broadcast_to(columns[:, 0:1], (tokens, heads * width))
    for head in range(1, heads):
        spread = jnp.where(lane == head, columns[:, head : head + 1], spread)
    return spread


def local_kernel(
    sections, x_ref, g_ref, write_ref, read_ref, decay_ref, send_ref, rows_ref, cols_ref, weights_ref
):
    heads, tokens = decay_ref.shape
    channels = x_ref.shape[1]
    head_size = channels // heads
    chunk = channels // sections
    decay = jnp.concatenate([decay_ref[...], jnp.zeros((8 - heads, tokens), f32)], axis=0)
    row_id = lax.broadcasted_iota(jnp.int32, (tokens, tokens), 0)
    col_id = lax.broadcasted_iota(jnp.int32, (tokens, tokens), 1)
    upto = (row_id <= col_id).astype(f32).astype(bf16)
    first, rest = split(decay)
    rest_wide = decay - first.astype(f32)
    second, third = split(rest_wide)
    pieces = jnp.concatenate([first.astype(f32), second.astype(f32), third.astype(f32)], axis=0)
    summed = dot(pieces.astype(bf16), upto, ((1,), (0,)))
    cumul = summed[0:8] + summed[8:16] + summed[16:24]
    rows_ref[...] = cumul
    cols = cumul.T
    cols_ref[...] = cols
    last = cols[tokens - 1 : tokens, :]
    lead = jnp.exp(cols)
    tail = jnp.exp(last - cols)
    weights_ref[...] = jnp.concatenate([lead, tail], axis=1)
    total = jnp.exp(last)
    x_turned = x_ref[...].T
    g_turned = g_ref[...].T
    write = write_ref[...].astype(f32)
    read = read_ref[...].astype(f32)
    per_head = head_size // chunk
    for head in range(heads):
        own = slice(head * head_size, (head + 1) * head_size)
        state = dot(
            x_turned[own],
            jnp.concatenate(split(write * tail[:, head : head + 1]), axis=1),
            ((1,), (0,)),
        )
        grad = dot(
            g_turned[own],
            jnp.concatenate(split(read * lead[:, head : head + 1]), axis=1),
            ((1,), (0,)),
        )
        width = state.shape[1] // 2
        state = state[:, :width] + state[:, width:]
        grad = grad[:, :width] + grad[:, width:]
        total_row = jnp.broadcast_to(total[:, head : head + 1], (1, width))
        for part in range(per_head):
            base = (head * per_head + part) * (2 * chunk + 1)
            at = slice(part * chunk, (part + 1) * chunk)
            send_ref[base : base + chunk, :] = state[at]
            send_ref[base + chunk : base + 2 * chunk, :] = grad[at]
            send_ref[base + 2 * chunk : base + 2 * chunk + 1, :] = total_row


def scan_kernel(sections, chunk, got_ref, out_ref):
    stride = 2 * chunk + 1

    def total(section):
        base = section * stride + 2 * chunk
        return got_ref[base : base + 1, :]

    running = jnp.zeros((chunk, got_ref.shape[1]), f32)
    for section in range(sections):
        base = section * stride
        out_ref[section, 0:chunk, :] = running
        running = total(section) * running + got_ref[base : base + chunk, :]
    running = jnp.zeros((chunk, got_ref.shape[1]), f32)
    for section in range(sections - 1, -1, -1):
        base = section * stride + chunk
        out_ref[section, chunk : 2 * chunk, :] = running
        running = total(section) * running + got_ref[base : base + chunk, :]


def intra_kernel(
    heads, x_ref, g_ref, write_ref, read_ref, rows_ref, cols_ref, y_ref, dx_ref, grad_ref
):
    tokens, channels = x_ref.shape
    head_size = channels // heads
    width = write_ref.shape[1]
    blocks = tokens // BLOCK
    y_ref[...] = jnp.zeros_like(y_ref)
    dx_ref[...] = jnp.zeros_like(dx_ref)
    grad_ref[...] = jnp.zeros_like(grad_ref)
    causal = lax.broadcasted_iota(jnp.int32, (BLOCK, BLOCK), 0) >= lax.broadcasted_iota(
        jnp.int32, (BLOCK, BLOCK), 1
    )
    for later in range(blocks):
        t = slice(later * BLOCK, (later + 1) * BLOCK)
        read = read_ref[t, :]
        g_block = g_ref[t, :]
        for earlier in range(later + 1):
            j = slice(earlier * BLOCK, (earlier + 1) * BLOCK)
            write = write_ref[j, :]
            x_block = x_ref[j, :]
            scores = dot(read, write, ((1,), (1,)))
            score_grad = jnp.zeros((BLOCK, BLOCK), f32)
            for head in range(heads):
                own = slice(head * head_size, (head + 1) * head_size)
                differ = cols_ref[t, head : head + 1] - rows_ref[head : head + 1, j]
                if later == earlier:
                    differ = jnp.where(causal, differ, -jnp.inf)
                decay = jnp.exp(differ)
                mixing = (scores * decay).astype(bf16)
                x_head = x_block[:, own]
                g_head = g_block[:, own]
                y_ref[t, own] += dot(mixing, x_head, ((1,), (0,)))
                dx_ref[j, own] += dot(mixing, g_head, ((0,), (0,)))
                score_grad += dot(g_head, x_head, ((1,), (1,))) * decay
            high, low = split(score_grad)
            grad_ref[j, 0:width] += dot(high, read, ((0,), (0,))) + dot(low, read, ((0,), (0,)))
            grad_ref[t, width:] += dot(high, write, ((1,), (0,))) + dot(low, write, ((1,), (0,)))


def states_of(state_ref, chunk):
    forward = state_ref[:, 0:chunk, :]
    backward = state_ref[:, chunk:, :]
    flat = (forward.shape[0] * chunk, forward.shape[2])
    return forward.reshape(flat), backward.reshape(flat)


def carried(values, state, columns, heads):
    rows, width = state.shape
    row_head = lax.broadcasted_iota(jnp.int32, (rows, 1), 0) // (rows // heads)
    total = None
    for head in range(heads):
        mine = jnp.where(row_head == head, state, 0.0)
        product = dot(values, jnp.concatenate(split(mine), axis=1), ((1,), (0,)))
        product = (product[:, :width] + product[:, width:]) * columns[:, head : head + 1]
        total = product if total is None else total + product
    return total


def carry_kernel(heads, chunk, group, core_ref, state_ref, x_ref, g_ref, weights_ref, intra_ref, keep_ref, send_ref):
    forward, backward = states_of(state_ref, chunk)
    width = forward.shape[1]
    count = keep_ref.shape[0]
    lead = weights_ref[:, 0:8]
    tail = weights_ref[:, 8:16]
    of_write = carried(x_ref[...], backward, tail, heads) + intra_ref[:, 0:width]
    of_read = carried(g_ref[...], forward, lead, heads) + intra_ref[:, width:]
    whole = jnp.concatenate([of_write, of_read], axis=1).reshape(count, 2, group, 2 * width)

    @pl.when(core_ref[0] == 0)
    def _():
        keep_ref[...] = whole[:, 0]
        send_ref[...] = whole[:, 1]

    @pl.when(core_ref[0] != 0)
    def _():
        keep_ref[...] = whole[:, 1]
        send_ref[...] = whole[:, 0]


def finish_kernel(
    heads, chunk, state_ref, write_ref, read_ref, weights_ref, y_ref, dx_ref, out_ref, dout_ref
):
    forward, backward = states_of(state_ref, chunk)
    head_size = forward.shape[0] // heads
    read, write = read_ref[...], write_ref[...]

    def inter(tokens, state):
        return dot(
            jnp.concatenate([tokens, tokens], axis=1),
            jnp.concatenate(split(state), axis=1),
            ((1,), (1,)),
        )

    lead = lanes_of_heads(weights_ref[:, 0:8], heads, head_size)
    out_ref[...] = (y_ref[...] + inter(read, forward) * lead).astype(bf16)
    tail = lanes_of_heads(weights_ref[:, 8:16], heads, head_size)
    dout_ref[...] = (dx_ref[...] + inter(write, backward) * tail).astype(bf16)


def call(kernel, outs, name, count, cost):
    return pl.pallas_call(
        kernel,
        out_shape=[jax.ShapeDtypeStruct(shape, dtype) for shape, dtype in outs],
        in_specs=[VMEM] * count if isinstance(count, int) else count,
        out_specs=[VMEM] * len(outs),
        compiler_params=pltpu.CompilerParams(vmem_limit_bytes=40 * 2**20),
        cost_estimate=pl.CostEstimate(flops=cost, bytes_accessed=4 * 2**20, transcendentals=0),
        name=name,
    )


def per_device(sections, spread, inputs, log_decay, write_proj, read_proj, grad_out):
    tokens, channels = inputs.shape
    heads = log_decay.shape[0]
    width = write_proj.shape[1]
    chunk = channels // sections
    stride = 2 * chunk + 1
    group = tokens // (2 * spread)
    send, rows, cols, weights = call(
        functools.partial(local_kernel, sections),
        [((sections * stride, width), f32), ((8, tokens), f32), ((tokens, 8), f32), ((tokens, 16), f32)],
        "local",
        5,
        10**9,
    )(inputs, grad_out, write_proj, read_proj, log_decay)
    got = lax.all_to_all(send.reshape(sections, stride, 1, width), ("x", "zh"), 0, 0)
    got = got.reshape(sections * stride, width)
    y_intra, dx_intra, grad_intra = call(
        functools.partial(intra_kernel, heads),
        [((tokens, channels), f32), ((tokens, channels), f32), ((tokens, 2 * width), f32)],
        "intra",
        6,
        8 * 10**9,
    )(inputs, grad_out, write_proj, read_proj, rows, cols)
    (states,) = call(
        functools.partial(scan_kernel, sections, chunk),
        [((sections, 2 * chunk, width), f32)],
        "scan",
        1,
        10**8,
    )(got)
    mine = lax.all_to_all(states, ("x", "zh"), 0, 0)
    core = lax.axis_index("core").reshape(1)
    keep, away = call(
        functools.partial(carry_kernel, heads, chunk, group),
        [((spread, group, 2 * width), f32)] * 2,
        "carry",
        [SMEM] + [VMEM] * 5,
        10**9,
    )(core, mine, inputs, grad_out, weights, grad_intra)
    other = lax.ppermute(away, "core", [(0, 1), (1, 0)])
    parts = lax.all_to_all(keep + other, ("y", "zl"), 0, 0)
    outputs, grad_inputs = call(
        functools.partial(finish_kernel, heads, chunk),
        [((tokens, channels), bf16)] * 2,
        "finish",
        6,
        2 * 10**9,
    )(mine, write_proj, read_proj, weights, y_intra, dx_intra)
    summed = jnp.sum(parts, axis=0)
    return (outputs, grad_inputs, summed[:, :width], summed[:, width:])


def solution(mesh, shape=(8, 4, 8, 2, 2)):
    axes = ("x", "zh", "y", "zl", "core")
    fine = Mesh(mesh.devices.reshape(shape), axes)
    seq, head = axes[:2], axes[2:]
    return jax.shard_map(
        functools.partial(per_device, shape[0] * shape[1], shape[2] * shape[3]),
        mesh=fine,
        in_specs=(P(seq, head), P(head, seq), P(seq, None), P(seq, None), P(seq, head)),
        out_specs=(P(seq, head), P(seq, head), P(axes, None), P(axes, None)),
        check_vma=False,
    )
```

time: 420 us -> 94.4 us (0.22)
  the two profiles are of different devices: /device:TPU:12 before, /device:TPU:2 now
where the time goes in v1:
time: 94.4 us; the launch traced here: 93.8 us
  starting transfers between devices  37.3 us (40%)
  waiting for transfers between devices  35.4 us (38%)
  Pallas kernels  12.6 us (13%)
  local copies, waits for them, and re-layouts  6.97 us (7%)
    all_to_all x1, starting transfers between devices, per_device(): lax.all_to_all(send.reshape(sections, stride, 1, width), ('x', 'zh'), 0, 0)  21.5 us
    all_to_all x1, waiting for transfers between devices, per_device(): lax.all_to_all(send.reshape(sections, stride, 1, width), ('x', 'zh'), 0, 0)  14.8 us
    all_to_all x1, waiting for transfers between devices, per_device(): parts = lax.all_to_all(keep + other, ('y', 'zl'), 0, 0)  13.2 us
    all_to_all x1, starting transfers between devices, per_device(): parts = lax.all_to_all(keep + other, ('y', 'zl'), 0, 0)  9.46 us
    pallas_call x1, Pallas kernels, per_device(): call(functools.partial(intra_kernel, heads), [((tokens, channels), f32),...  6.62 us
    unnamed x26, local copies, waits for them, and re-layouts  6.36 us
    all_to_all x1, waiting for transfers between devices, per_device(): mine = lax.all_to_all(states, ('x', 'zh'), 0, 0)  5.65 us
    all_to_all x1, starting transfers between devices, per_device(): mine = lax.all_to_all(states, ('x', 'zh'), 0, 0)  4.42 us
  transfers between devices with their start and end apart: 4, of which 4 were waited for; matrix products, arithmetic and copies ran while one was open for 0% of the time, Pallas kernels for 9%

profile of v1, /device:TPU:2, one launch (start us, length us, event | category | flops | bytes accessed | tf_op | source)
XLA Modules:
  0.0 93.8 jit_solution(3572550454833084075)
XLA Ops:
  0.6 0.0 copy-start
  0.6 1.0 %copy-done = bf16[768,256]{1,0:T(8,128)(2,1)S(1)} copy-done((bf16[768,256]{1,0:T(8,128)(2,1)S(1)}, bf16[768,256]{1,0:T(8,128)(2,1)}, u32[]{:S(2)}) %copy-start) | copy-done | bytes 393240
  1.6 1.0 %copy-done.2 = bf16[768,256]{1,0:T(8,128)(2,1)S(1)} copy-done((bf16[768,256]{1,0:T(8,128)(2,1)S(1)}, bf16[768,256]{1,0:T(8,128)(2,1)}, u32[]{:S(2)}) %copy-start.2) | copy-done | bytes 393240
  2.6 0.9 copy-done.4
  3.6 0.9 copy-done.6
  4.5 0.7 copy-done.8
  5.2 2.3 %local.1 = (f32[544,128]{1,0:T(8,128)}, f32[8,768]{1,0:T(8,128)S(1)}, f32[768,8]{1,0:T(8,128)S(1)}, f32[768,16]{1,0:T(8,128)S(1)}) custom-call(bf16[768,256]{1,0:T(8,128)(2,1)S(1)} %copy-done, bf16[768,256]{1,0:T(8,128)(2,1)S(1)} %copy-done.2, bf16[768,128]{1,0:T(8,128)(2,1)S(1)} %copy-done.4, bf16[768,128]{1,0:T(8,128)(2,1)S(1)} %copy-done.6, ...), custom_call_target="tpu_custom_call" | custom-call | flops 1000000000 | bytes 4194304 | tf_op jit(solution)/shard_map/local/pallas_call | solution.py:227
  7.5 21.5 %all-to-all-start = ((f32[32,17,1,128]{3,2,1,0:T(1,128)}), f32[32,17,1,128]{3,2,1,0:T(1,128)S(1)}, u32[]{:S(2)}, u32[]{:S(2)}) async-start(f32[32,17,1,128]{3,2,1,0:T(1,128)} %bitcast), calls=%async_computation | async-start | bytes 557056 | tf_op jit(solution)/shard_map/all_to_all | solution.py:234
  29.0 14.8 %all-to-all-done = f32[32,17,1,128]{3,2,1,0:T(1,128)S(1)} async-done(((f32[32,17,1,128]{3,2,1,0:T(1,128)}), f32[32,17,1,128]{3,2,1,0:T(1,128)S(1)}, u32[]{:S(2)}, u32[]{:S(2)}) %all-to-all-start) | async-done | bytes 278560 | tf_op jit(solution)/shard_map/all_to_all | solution.py:234
  43.9 0.8 scan.1
  44.7 4.4 %all-to-all-start.1 = ((f32[32,16,128]{2,1,0:T(8,128)}), f32[32,16,128]{2,1,0:T(8,128)S(1)}, u32[]{:S(2)}, u32[]{:S(2)}) async-start(f32[32,16,128]{2,1,0:T(8,128)} %scan.1), calls=%async_computation.1 | async-start | bytes 524288 | tf_op jit(solution)/shard_map/all_to_all | solution.py:250
  49.1 0.0 copy-done.7
  49.1 6.6 %intra.1 = (f32[768,256]{1,0:T(8,128)S(1)}, f32[768,256]{1,0:T(8,128)S(1)}, f32[768,256]{1,0:T(8,128)S(1)}) custom-call(bf16[768,256]{1,0:T(8,128)(2,1)S(1)} %copy-done.1, bf16[768,256]{1,0:T(8,128)(2,1)S(1)} %copy-done.3, bf16[768,128]{1,0:T(8,128)(2,1)S(1)} %copy-done.5, bf16[768,128]{1,0:T(8,128)(2,1)S(1)} %copy-done.7, ...), custom_call_target="tpu_custom_call" | custom-call | flops 8000000000 | bytes 4194304 | tf_op jit(solution)/shard_map/intra/pallas_call | solution.py:236
  55.8 0.9 copy-done.9
  56.7 0.9 copy-done.11
  57.6 5.7 %all-to-all-done.1.state_ref = f32[32,16,128]{2,1,0:T(8,128)S(1)} async-done(((f32[32,16,128]{2,1,0:T(8,128)}), f32[32,16,128]{2,1,0:T(8,128)S(1)}, u32[]{:S(2)}, u32[]{:S(2)}) %all-to-all-start.1) | async-done | bytes 262176 | tf_op jit(solution)/shard_map/all_to_all | solution.py:250
  63.2 1.1 %carry.1 = (f32[16,24,256]{2,1,0:T(8,128)S(1)}, f32[16,24,256]{2,1,0:T(8,128)S(1)}) custom-call(s32[1]{0:T(128)} %bitcast.2.core_ref, f32[32,16,128]{2,1,0:T(8,128)S(1)} %all-to-all-done.1.state_ref, bf16[768,256]{1,0:T(8,128)(2,1)S(1)} %copy-done.1, bf16[768,256]{1,0:T(8,128)(2,1)S(1)} %copy-done.3, f32[768,16]{1,0:T(8,128)S(1)} %get-tuple-element.16.weights_ref, ...), custom_call_target="tpu_custom_call" | custom-call | flops 1000000000 | bytes 4194304 | tf_op jit(solution)/shard_map/carry/pallas_call | solution.py:252
  64.3 1.9 %collective-permute-start = (f32[16,24,256]{2,1,0:T(8,128)S(1)}, f32[16,24,256]{2,1,0:T(8,128)S(1)}, u32[]{:S(2)}, u32[]{:S(2)}) collective-permute-start(f32[16,24,256]{2,1,0:T(8,128)S(1)} %get-tuple-element.25), channel_id=1, source_target_pairs={{0,1},{1,0},{2,3},{3,2},{4,5},{5,4},{6,7},{7,6},{8,9},{9,8},{10,11... | collective-permute-start | bytes 1179656 | tf_op jit(solution)/shard_map/ppermute | solution.py:259
  66.2 1.7 %collective-permute-done = f32[16,24,256]{2,1,0:T(8,128)S(1)} collective-permute-done((f32[16,24,256]{2,1,0:T(8,128)S(1)}, f32[16,24,256]{2,1,0:T(8,128)S(1)}, u32[]{:S(2)}, u32[]{:S(2)}) %collective-permute-start) | collective-permute-done | bytes 393248 | tf_op jit(solution)/shard_map/ppermute | solution.py:259
  67.9 0.8 add.3
  68.7 9.5 %all-to-all-start.2 = ((f32[16,24,256]{2,1,0:T(8,128)}), f32[16,24,256]{2,1,0:T(8,128)S(1)}, u32[]{:S(2)}, u32[]{:S(2)}) async-start(f32[16,24,256]{2,1,0:T(8,128)} %add.3), calls=%async_computation.2 | async-start | bytes 786432 | tf_op jit(solution)/shard_map/all_to_all | solution.py:260
  78.2 1.8 %finish.1 = (bf16[768,256]{1,0:T(8,128)(2,1)}, bf16[768,256]{1,0:T(8,128)(2,1)}) custom-call(f32[32,16,128]{2,1,0:T(8,128)S(1)} %all-to-all-done.1.state_ref, bf16[768,128]{1,0:T(8,128)(2,1)S(1)} %copy-done.5, bf16[768,128]{1,0:T(8,128)(2,1)S(1)} %copy-done.7, f32[768,16]{1,0:T(8,128)S(1)} %get-tuple-element.16.weights_ref, f32[768,256]{1,0:T(8,128)S(1)} %copy-done.10, ...), custom_call_target="tpu_custom_call" | custom-call | flops 2000000000 | bytes 4194304 | tf_op jit(solution)/shard_map/finish/pallas_call | solution.py:261
  80.0 13.2 %all-to-all-done.2 = f32[16,24,256]{2,1,0:T(8,128)S(1)} async-done(((f32[16,24,256]{2,1,0:T(8,128)}), f32[16,24,256]{2,1,0:T(8,128)S(1)}, u32[]{:S(2)}, u32[]{:S(2)}) %all-to-all-start.2) | async-done | bytes 393248 | tf_op jit(solution)/shard_map/all_to_all | solution.py:260
  93.2 0.6 fusion
  (18 shorter events, 0.1 us)
Async XLA Ops:
  0.6 1.0 %copy-start = (bf16[768,256]{1,0:T(8,128)(2,1)S(1)}, bf16[768,256]{1,0:T(8,128)(2,1)}, u32[]{:S(2)}) copy-start(bf16[768,256]{1,0:T(8,128)(2,1)} %x_ref.5) | copy-start | bytes 1179652
  1.6 1.0 %copy-start.2 = (bf16[768,256]{1,0:T(8,128)(2,1)S(1)}, bf16[768,256]{1,0:T(8,128)(2,1)}, u32[]{:S(2)}) copy-start(bf16[768,256]{1,0:T(8,128)(2,1)} %g_ref.5) | copy-start | bytes 1179652
  2.6 0.9 copy-start.4
  3.6 0.9 copy-start.6
  4.5 0.7 copy-start.8
  7.5 41.6 %copy-start.7 = (bf16[768,128]{1,0:T(8,128)(2,1)S(1)}, bf16[768,128]{1,0:T(8,128)(2,1)}, u32[]{:S(2)}) copy-start(bf16[768,128]{1,0:T(8,128)(2,1)} %read_ref.5) | copy-start | bytes 589828
  7.5 36.4 %all-to-all-start = ((f32[32,17,1,128]{3,2,1,0:T(1,128)}), f32[32,17,1,128]{3,2,1,0:T(1,128)S(1)}, u32[]{:S(2)}, u32[]{:S(2)}) async-start(f32[32,17,1,128]{3,2,1,0:T(1,128)} %bitcast), calls=%async_computation | async-start | bytes 557056 | tf_op jit(solution)/shard_map/all_to_all | solution.py:234
  43.9 5.2 %copy-start.3 = (bf16[768,256]{1,0:T(8,128)(2,1)S(1)}, bf16[768,256]{1,0:T(8,128)(2,1)}, u32[]{:S(2)}) copy-start(bf16[768,256]{1,0:T(8,128)(2,1)} %g_ref.5) | copy-start | bytes 1179652
  43.9 5.2 %copy-start.5 = (bf16[768,128]{1,0:T(8,128)(2,1)S(1)}, bf16[768,128]{1,0:T(8,128)(2,1)}, u32[]{:S(2)}) copy-start(bf16[768,128]{1,0:T(8,128)(2,1)} %write_ref.5) | copy-start | bytes 589828
  44.7 4.5 %copy-start.1 = (bf16[768,256]{1,0:T(8,128)(2,1)S(1)}, bf16[768,256]{1,0:T(8,128)(2,1)}, u32[]{:S(2)}) copy-start(bf16[768,256]{1,0:T(8,128)(2,1)} %x_ref.5) | copy-start | bytes 1179652
  44.7 18.5 %all-to-all-start.1 = ((f32[32,16,128]{2,1,0:T(8,128)}), f32[32,16,128]{2,1,0:T(8,128)S(1)}, u32[]{:S(2)}, u32[]{:S(2)}) async-start(f32[32,16,128]{2,1,0:T(8,128)} %scan.1), calls=%async_computation.1 | async-start | bytes 524288 | tf_op jit(solution)/shard_map/all_to_all | solution.py:250
  55.8 0.9 copy-start.9
  56.7 0.9 copy-start.11
  64.3 3.6 %collective-permute-start = (f32[16,24,256]{2,1,0:T(8,128)S(1)}, f32[16,24,256]{2,1,0:T(8,128)S(1)}, u32[]{:S(2)}, u32[]{:S(2)}) collective-permute-start(f32[16,24,256]{2,1,0:T(8,128)S(1)} %get-tuple-element.25), channel_id=1, source_target_pairs={{0,1},{1,0},{2,3},{3,2},{4,5},{5,4},{6,7},{7,6},{8,9},{9,8},{10,11... | collective-permute-start | bytes 1179656 | tf_op jit(solution)/shard_map/ppermute | solution.py:259
  67.9 10.3 %copy-start.10 = (f32[768,256]{1,0:T(8,128)S(1)}, f32[768,256]{1,0:T(8,128)}, u32[]{:S(2)}) copy-start(f32[768,256]{1,0:T(8,128)} %copy-done.9) | copy-start | bytes 2359300
  67.9 10.3 %copy-start.12 = (f32[768,256]{1,0:T(8,128)S(1)}, f32[768,256]{1,0:T(8,128)}, u32[]{:S(2)}) copy-start(f32[768,256]{1,0:T(8,128)} %copy-done.11) | copy-start | bytes 2359300
  68.7 24.4 %all-to-all-start.2 = ((f32[16,24,256]{2,1,0:T(8,128)}), f32[16,24,256]{2,1,0:T(8,128)S(1)}, u32[]{:S(2)}, u32[]{:S(2)}) async-start(f32[16,24,256]{2,1,0:T(8,128)} %add.3), calls=%async_computation.2 | async-start | bytes 786432 | tf_op jit(solution)/shard_map/all_to_all | solution.py:260

commit v2 on v1

v2 whole, which is shorter than its diff:
```python
import functools

import jax
import jax.numpy as jnp
from jax import lax
from jax.experimental import pallas as pl
from jax.experimental.pallas import tpu as pltpu
from jax.sharding import Mesh, PartitionSpec as P

f32 = jnp.float32
bf16 = jnp.bfloat16
VMEM = pl.BlockSpec(memory_space=pltpu.VMEM)
SMEM = pl.BlockSpec(memory_space=pltpu.SMEM)
ANY = pl.BlockSpec(memory_space=pl.ANY)
BLOCK = 256


def dot(a, b, dims):
    return lax.dot_general(a, b, (dims, ((), ())), preferred_element_type=f32)


def split(value):
    high = value.astype(bf16)
    return high, (value - high.astype(f32)).astype(bf16)


def lanes_of_heads(columns, heads, width):
    tokens = columns.shape[0]
    lane = lax.broadcasted_iota(jnp.int32, (tokens, heads * width), 1) // width
    spread = jnp.broadcast_to(columns[:, 0:1], (tokens, heads * width))
    for head in range(1, heads):
        spread = jnp.where(lane == head, columns[:, head : head + 1], spread)
    return spread


def local_kernel(
    sections,
    x_hbm,
    g_hbm,
    write_hbm,
    read_hbm,
    decay_hbm,
    send_ref,
    rows_ref,
    cols_ref,
    x_ref,
    g_ref,
    write_ref,
    read_ref,
    decay_ref,
    arrived,
):
    pairs = (
        (decay_hbm, decay_ref),
        (x_hbm, x_ref),
        (write_hbm, write_ref),
        (g_hbm, g_ref),
        (read_hbm, read_ref),
    )
    copies = [
        pltpu.make_async_copy(source, target, arrived.at[at])
        for at, (source, target) in enumerate(pairs)
    ]
    for copy in copies:
        copy.start()
    heads, tokens = decay_ref.shape
    channels = x_ref.shape[1]
    head_size = channels // heads
    chunk = channels // sections
    lanes = 128
    upto = (
        lax.broadcasted_iota(jnp.int32, (lanes, lanes), 0)
        <= lax.broadcasted_iota(jnp.int32, (lanes, lanes), 1)
    ).astype(f32).astype(bf16)
    copies[0].wait()
    decay = jnp.concatenate([decay_ref[...], jnp.zeros((8 - heads, tokens), f32)], axis=0)
    first, _ = split(decay)
    second, third = split(decay - first.astype(f32))
    wide = jnp.concatenate([first.astype(f32), second.astype(f32), third.astype(f32)], axis=0)
    count = tokens // lanes
    stacked = jnp.concatenate(
        [wide[:, part * lanes : (part + 1) * lanes] for part in range(count)], axis=0
    ).astype(bf16)
    summed = dot(stacked, upto, ((1,), (0,)))
    parts = []
    before = jnp.zeros((8, 1), f32)
    for part in range(count):
        base = 24 * part
        inside = summed[base : base + 8] + summed[base + 8 : base + 16] + summed[base + 16 : base + 24]
        parts.append(inside + before)
        before = before + inside[:, lanes - 1 : lanes]
    cumul = jnp.concatenate(parts, axis=1)
    rows_ref[...] = cumul
    total = jnp.exp(before)
    cols = jnp.concatenate([cumul, jnp.exp(cumul), jnp.exp(before - cumul)], axis=0).T
    cols_ref[...] = cols
    per_head = head_size // chunk
    for flow, (values_ref, vectors_ref, column) in enumerate(
        ((x_ref, write_ref, 16), (g_ref, read_ref, 8))
    ):
        copies[1 + 2 * flow].wait()
        turned = values_ref[...].T
        copies[2 + 2 * flow].wait()
        vectors = vectors_ref[...].astype(f32)
        width = vectors.shape[1]
        for head in range(heads):
            state = dot(
                turned[head * head_size : (head + 1) * head_size],
                jnp.concatenate(split(vectors * cols[:, column + head : column + head + 1]), axis=1),
                ((1,), (0,)),
            )
            state = state[:, :width] + state[:, width:]
            for part in range(per_head):
                base = (head * per_head + part) * (2 * chunk + 1)
                at = base + flow * chunk
                send_ref[at : at + chunk, :] = state[part * chunk : (part + 1) * chunk]
                if flow == 0:
                    at = base + 2 * chunk
                    send_ref[at : at + 1, :] = jnp.broadcast_to(total[head : head + 1], (1, width))


def scan_kernel(sections, chunk, got_ref, cross_ref, out_ref, crossed_ref):
    stride = 2 * chunk + 1

    def total(section):
        base = section * stride + 2 * chunk
        return got_ref[base : base + 1, :]

    running = jnp.zeros((chunk, got_ref.shape[1]), f32)
    for section in range(sections):
        base = section * stride
        out_ref[section, 1] = running
        running = total(section) * running + got_ref[base : base + chunk, :]
    running = jnp.zeros((chunk, got_ref.shape[1]), f32)
    for section in range(sections - 1, -1, -1):
        base = section * stride + chunk
        out_ref[section, 0] = running
        running = total(section) * running + got_ref[base : base + chunk, :]


def intra_kernel(
    heads,
    core_ref,
    x_ref,
    g_ref,
    write_ref,
    read_ref,
    rows_ref,
    cols_ref,
    y_ref,
    dx_ref,
    own_ref,
    cross_ref,
    grad_ref,
):
    tokens, channels = x_ref.shape
    head_size = channels // heads
    width = write_ref.shape[1]
    blocks = tokens // BLOCK
    y_ref[...] = jnp.zeros_like(y_ref)
    dx_ref[...] = jnp.zeros_like(dx_ref)
    grad_ref[...] = jnp.zeros_like(grad_ref)
    causal = lax.broadcasted_iota(jnp.int32, (BLOCK, BLOCK), 0) >= lax.broadcasted_iota(
        jnp.int32, (BLOCK, BLOCK), 1
    )
    for later in range(blocks):
        t = slice(later * BLOCK, (later + 1) * BLOCK)
        read = read_ref[t, :]
        g_block = g_ref[t, :]
        for earlier in range(later + 1):
            j = slice(earlier * BLOCK, (earlier + 1) * BLOCK)
            write = write_ref[j, :]
            x_block = x_ref[j, :]
            scores = dot(read, write, ((1,), (1,)))
            score_grad = jnp.zeros((BLOCK, BLOCK), f32)
            for head in range(heads):
                own = slice(head * head_size, (head + 1) * head_size)
                differ = cols_ref[t, head : head + 1] - rows_ref[head : head + 1, j]
                if later == earlier:
                    differ = jnp.where(causal, differ, -jnp.inf)
                decay = jnp.exp(differ)
                mixing = (scores * decay).astype(bf16)
                x_head = x_block[:, own]
                g_head = g_block[:, own]
                y_ref[t, own] += dot(mixing, x_head, ((1,), (0,)))
                dx_ref[j, own] += dot(mixing, g_head, ((0,), (0,)))
                score_grad += dot(g_head, x_head, ((1,), (1,))) * decay
            high, low = split(score_grad)
            grad_ref[j, 0:width] += dot(high, read, ((0,), (0,))) + dot(low, read, ((0,), (0,)))
            grad_ref[t, width:] += dot(high, write, ((1,), (0,))) + dot(low, write, ((1,), (0,)))
    first = core_ref[0] == 0
    own_ref[:, channels:] = jnp.where(first, grad_ref[:, 0:width], grad_ref[:, width:])
    cross_ref[:, channels:] = jnp.where(first, grad_ref[:, width:], grad_ref[:, 0:width])
    x_weighted = x_ref[...].astype(f32) * lanes_of_heads(cols_ref[:, 16:24], heads, head_size)
    g_weighted = g_ref[...].astype(f32) * lanes_of_heads(cols_ref[:, 8:16], heads, head_size)
    own_ref[:, 0:channels] = jnp.where(first, x_weighted, g_weighted)
    cross_ref[:, 0:channels] = jnp.where(first, g_weighted, x_weighted)


def carry_kernel(core_ref, state_ref, own_ref, other_ref, out_ref, kept_ref, swap_ref):
    core = core_ref[0]
    channels = own_ref.shape[1] - out_ref.shape[1]
    width = out_ref.shape[1]
    flat = (channels, width)
    mine = state_ref[:, pl.ds(core, 1)].reshape(flat)
    partner = state_ref[:, pl.ds(1 - core, 1)].reshape(flat)
    kept_ref[...] = mine
    swap_ref[...] = partner
    total = own_ref[:, channels:] + other_ref[:, channels:]
    for values_ref, state in ((own_ref, mine), (other_ref, partner)):
        high, low = split(values_ref[:, 0:channels])
        state_high, state_low = split(state)
        product = dot(high, jnp.concatenate([state_high, state_low], axis=1), ((1,), (0,)))
        total += product[:, :width] + product[:, width:] + dot(low, state_high, ((1,), (0,)))
    out_ref[...] = total


def finish_kernel(
    heads, core_ref, kept_ref, came_ref, write_ref, read_ref, cols_ref, y_ref, dx_ref, out_ref, dout_ref
):
    first = core_ref[0] == 0
    forward = jnp.where(first, came_ref[...], kept_ref[...])
    backward = jnp.where(first, kept_ref[...], came_ref[...])
    head_size = forward.shape[0] // heads
    read, write = read_ref[...], write_ref[...]

    def inter(tokens, state):
        return dot(
            jnp.concatenate([tokens, tokens], axis=1),
            jnp.concatenate(split(state), axis=1),
            ((1,), (1,)),
        )

    lead = lanes_of_heads(cols_ref[:, 8:16], heads, head_size)
    out_ref[...] = (y_ref[...] + inter(read, forward) * lead).astype(bf16)
    tail = lanes_of_heads(cols_ref[:, 16:24], heads, head_size)
    dout_ref[...] = (dx_ref[...] + inter(write, backward) * tail).astype(bf16)


def call(kernel, outs, specs, cost, mebibytes, scratch=(), out_specs=None, **more):
    return pl.pallas_call(
        kernel,
        out_shape=[jax.ShapeDtypeStruct(shape, dtype) for shape, dtype in outs],
        in_specs=specs,
        out_specs=out_specs or [VMEM] * len(outs),
        scratch_shapes=list(scratch),
        compiler_params=pltpu.CompilerParams(vmem_limit_bytes=mebibytes * 2**20),
        cost_estimate=pl.CostEstimate(flops=cost, bytes_accessed=4 * 2**20, transcendentals=0),
        **more,
    )


def per_device(sections, spread, inputs, log_decay, write_proj, read_proj, grad_out):
    tokens, channels = inputs.shape
    heads = log_decay.shape[0]
    width = write_proj.shape[1]
    chunk = channels // sections
    stride = 2 * chunk + 1
    core = lax.axis_index("core").reshape(1)
    swap_cores = [(0, 1), (1, 0)]
    send, rows, cols = call(
        functools.partial(local_kernel, sections),
        [((sections * stride, width), f32), ((8, tokens), f32), ((tokens, 24), f32)],
        [ANY] * 5,
        10**9,
        60,
        [
            pltpu.VMEM(inputs.shape, bf16),
            pltpu.VMEM(inputs.shape, bf16),
            pltpu.VMEM(write_proj.shape, bf16),
            pltpu.VMEM(write_proj.shape, bf16),
            pltpu.VMEM(log_decay.shape, f32),
            pltpu.SemaphoreType.DMA((5,)),
        ],
    )(inputs, grad_out, write_proj, read_proj, log_decay)
    got = lax.all_to_all(send.reshape(sections, stride, 1, width), ("x", "zh"), 0, 0)
    got = got.reshape(sections * stride, width)
    y_intra, dx_intra, own, cross = call(
        functools.partial(intra_kernel, heads),
        [
            ((tokens, channels), f32),
            ((tokens, channels), f32),
            ((tokens, channels + width), f32),
            ((tokens, channels + width), f32),
        ],
        [SMEM] + [VMEM] * 6,
        8 * 10**9,
        16,
        [pltpu.VMEM((tokens, 2 * width), f32)],
    )(core, inputs, grad_out, write_proj, read_proj, rows, cols)
    states, cross = call(
        functools.partial(scan_kernel, sections, chunk),
        [((sections, 2, chunk, width), f32), (cross.shape, f32)],
        [VMEM, ANY],
        10**8,
        4,
        out_specs=[VMEM, ANY],
        input_output_aliases={1: 1},
    )(got, cross)
    mine = lax.all_to_all(
        states.reshape(2 * sections, chunk, width), ("x", "zh", "core"), 0, 0
    ).reshape(sections, 2, chunk, width)
    other = lax.ppermute(cross, "core", swap_cores)
    piece, kept, swap = call(
        carry_kernel,
        [((tokens, width), f32), ((channels, width), f32), ((channels, width), f32)],
        [SMEM] + [VMEM] * 3,
        10**9,
        12,
    )(core, mine, own, other)
    parts = lax.all_to_all(
        piece.reshape(2 * spread, tokens // (2 * spread), width), ("y", "zl", "core"), 0, 0
    )
    came = lax.ppermute(swap, "core", swap_cores)
    outputs, grad_inputs = call(
        functools.partial(finish_kernel, heads),
        [((tokens, channels), bf16)] * 2,
        [SMEM] + [VMEM] * 7,
        2 * 10**9,
        12,
    )(core, kept, came, write_proj, read_proj, cols, y_intra, dx_intra)
    summed = jnp.sum(parts.reshape(spread, 2, -1, width), axis=0)
    return (outputs, grad_inputs, summed[0], summed[1])


def solution(mesh, shape=(8, 4, 8, 2, 2)):
    axes = ("x", "zh", "y", "zl", "core")
    fine = Mesh(mesh.devices.reshape(shape), axes)
    seq, head = axes[:2], axes[2:]
    return jax.shard_map(
        functools.partial(per_device, shape[0] * shape[1], shape[2] * shape[3]),
        mesh=fine,
        in_specs=(P(seq, head), P(head, seq), P(seq, None), P(seq, None), P(seq, head)),
        out_specs=(P(seq, head), P(seq, head), P(axes, None), P(axes, None)),
        check_vma=False,
    )
```

time: 94.4 us -> 94.1 us (level)
  the two profiles are of different devices: /device:TPU:2 before, /device:TPU:1 now
where the time goes in v2:
time: 94.1 us; the launch traced here: 93.6 us
  starting transfers between devices  37.9 us (40%)
  blocking collectives  25.1 us (27%)
  Pallas kernels  14.4 us (15%)
  waiting for transfers between devices  11.1 us (12%)
  local copies, waits for them, and re-layouts  4.29 us (5%)
    all_to_all x1, blocking collectives, per_device(): lax.all_to_all(states.reshape(2 * sections, chunk, width), ('x', 'zh', 'c...  25.1 us
    all_to_all x1, starting transfers between devices, per_device(): lax.all_to_all(send.reshape(sections, stride, 1, width), ('x', 'zh'), 0, 0)  21.6 us
    all_to_all x1, starting transfers between devices, per_device(): lax.all_to_all(piece.reshape(2 * spread, tokens // (2 * spread), width),...  9.79 us
    all_to_all x1, waiting for transfers between devices, per_device(): lax.all_to_all(piece.reshape(2 * spread, tokens // (2 * spread), width),...  8.72 us
    pallas_call x1, Pallas kernels, per_device(): call(functools.partial(intra_kernel, heads), [((tokens, channels), f32),...  7.53 us
    ppermute x1, starting transfers between devices, per_device(): other = lax.ppermute(cross, 'core', swap_cores)  4.35 us
    unnamed x22, local copies, waits for them, and re-layouts  3.68 us
    pallas_call x1, Pallas kernels, per_device(): call(functools.partial(local_kernel, sections), [((sections * stride, wid...  3.67 us
  transfers between devices with their start and end apart: 4, of which 3 were waited for; matrix products, arithmetic and copies ran while one was open for 0% of the time, Pallas kernels for 10%

profile of v2, /device:TPU:1, one launch (start us, length us, event | category | flops | bytes accessed | tf_op | source)
XLA Modules:
  0.0 93.6 jit_solution(12570552871045207933)
XLA Ops:
  0.6 0.0 copy-start.3
  0.6 0.0 copy-start.2
  0.7 0.0 copy-start.1
  0.7 0.0 copy-start
  0.7 3.7 %shard_map.84 = (f32[544,128]{1,0:T(8,128)}, f32[8,768]{1,0:T(8,128)}, f32[768,24]{1,0:T(8,128)}) custom-call(bf16[768,256]{1,0:T(8,128)(2,1)} %x_ref.1, bf16[768,256]{1,0:T(8,128)(2,1)} %g_ref.1, bf16[768,128]{1,0:T(8,128)(2,1)} %write_ref.3, bf16[768,128]{1,0:T(8,128)(2,1)} %read_ref.3, f32[4,768]{1,0:T(4,128)} %decay_hbm.1), custom_call_target="tpu_custom_call" | custom-call | flops 1000000000 | bytes 4194304 | tf_op jit(solution)/shard_map/pallas_call | solution.py:261
  4.3 21.6 %all-to-all-start = ((f32[32,17,1,128]{3,2,1,0:T(1,128)}), f32[32,17,1,128]{3,2,1,0:T(1,128)S(1)}, u32[]{:S(2)}, u32[]{:S(2)}) async-start(f32[32,17,1,128]{3,2,1,0:T(1,128)} %bitcast.15), calls=%async_computation | async-start | bytes 557056 | tf_op jit(solution)/shard_map/all_to_all | solution.py:276
  26.0 0.0 copy-start.6
  26.0 1.0 %copy-done.6 = f32[768,24]{1,0:T(8,128)S(1)} copy-done((f32[768,24]{1,0:T(8,128)S(1)}, f32[768,24]{1,0:T(8,128)}, u32[]{:S(2)}) %copy-start.6) | copy-done | bytes 73752
  27.0 0.7 copy-done.10
  27.8 7.5 %shard_map.85 = (f32[768,256]{1,0:T(8,128)S(1)}, f32[768,256]{1,0:T(8,128)S(1)}, f32[768,384]{1,0:T(8,128)S(1)}, f32[768,384]{1,0:T(8,128)S(1)}) custom-call(s32[1]{0:T(128)} %bitcast.core_ref, bf16[768,256]{1,0:T(8,128)(2,1)S(1)} %copy-done, bf16[768,256]{1,0:T(8,128)(2,1)S(1)} %copy-done.1, bf16[768,128]{1,0:T(8,128)(2,1)S(1)} %copy-done.2, ...), custom_call_target="tpu_custom_call" | custom-call | flops 8000000000 | bytes 4194304 | tf_op jit(solution)/shard_map/pallas_call | solution.py:278
  35.3 1.0 %copy-done.4 = f32[768,384]{1,0:T(8,128)} copy-done((f32[768,384]{1,0:T(8,128)}, f32[768,384]{1,0:T(8,128)S(1)}, u32[]{:S(2)}) %copy-start.4) | copy-done | bytes 1179672
  36.4 0.9 copy-done.8
  37.2 1.3 %all-to-all-done = f32[32,17,1,128]{3,2,1,0:T(1,128)S(1)} async-done(((f32[32,17,1,128]{3,2,1,0:T(1,128)}), f32[32,17,1,128]{3,2,1,0:T(1,128)S(1)}, u32[]{:S(2)}, u32[]{:S(2)}) %all-to-all-start) | async-done | bytes 278560 | tf_op jit(solution)/shard_map/all_to_all | solution.py:276
  38.5 0.1 shard_map.86
  38.6 4.4 %collective-permute-start = (f32[768,384]{1,0:T(8,128)S(1)}, f32[768,384]{1,0:T(8,128)S(1)}, u32[]{:S(2)}, u32[]{:S(2)}) collective-permute-start(f32[768,384]{1,0:T(8,128)S(1)} %get-tuple-element.24), channel_id=1, source_target_pairs={{0,1},{1,0},{2,3},{3,2},{4,5},{5,4},{6,7},{7,6},{8,9},{9,8},{10,11... | collective-permute-start | bytes 3538952 | tf_op jit(solution)/shard_map/ppermute | solution.py:303
  43.0 25.1 %all_to_all.15 = f32[64,8,128]{2,1,0:T(8,128)S(1)} all-to-all(f32[64,8,128]{2,1,0:T(8,128)S(1)} %bitcast.13), channel_id=1, replica_groups=mesh['x'=8,'zh'=4,'y'=8,'zl'=2,'core'=2] {'x','zh','core'}, dimensions={0} | all-to-all | bytes 524288 | tf_op jit(solution)/shard_map/all_to_all | solution.py:300
  68.1 0.0 collective-permute-done.other_ref
  68.1 1.3 %shard_map.87 = (f32[768,128]{1,0:T(8,128)}, f32[256,128]{1,0:T(8,128)S(1)}, f32[256,128]{1,0:T(8,128)S(1)}) custom-call(s32[1]{0:T(128)} %bitcast.core_ref, f32[32,2,8,128]{3,2,1,0:T(8,128)S(1)} %bitcast.12, f32[768,384]{1,0:T(8,128)S(1)} %copy-done.5, f32[768,384]{1,0:T(8,128)S(1)} %collective-permute-done.other_ref), custom_call_target="tpu_custom_call" | custom-call | flops 1000000000 | bytes 4194304 | tf_op jit(solution)/shard_map/pallas_call | solution.py:304
  69.4 9.8 %all-to-all-start.2 = ((f32[32,24,128]{2,1,0:T(8,128)}), f32[32,24,128]{2,1,0:T(8,128)S(1)}, u32[]{:S(2)}, u32[]{:S(2)}) async-start(f32[32,24,128]{2,1,0:T(8,128)} %bitcast.5), calls=%async_computation.2 | async-start | bytes 786432 | tf_op jit(solution)/shard_map/all_to_all | solution.py:311
  79.2 2.1 %collective-permute-start.1 = (f32[256,128]{1,0:T(8,128)S(1)}, f32[256,128]{1,0:T(8,128)S(1)}, u32[]{:S(2)}, u32[]{:S(2)}) collective-permute-start(f32[256,128]{1,0:T(8,128)S(1)} %get-tuple-element.26), channel_id=1, source_target_pairs={{0,1},{1,0},{2,3},{3,2},{4,5},{5,4},{6,7},{7,6},{8,9},{9,8},{10,11... | collective-permute-start | bytes 393224 | tf_op jit(solution)/shard_map/ppermute | solution.py:314
  81.4 1.1 %collective-permute-done.1.came_ref = f32[256,128]{1,0:T(8,128)S(1)} collective-permute-done((f32[256,128]{1,0:T(8,128)S(1)}, f32[256,128]{1,0:T(8,128)S(1)}, u32[]{:S(2)}, u32[]{:S(2)}) %collective-permute-start.1) | collective-permute-done | bytes 131104 | tf_op jit(solution)/shard_map/ppermute | solution.py:314
  82.5 1.8 %shard_map.88 = (bf16[768,256]{1,0:T(8,128)(2,1)}, bf16[768,256]{1,0:T(8,128)(2,1)}) custom-call(s32[1]{0:T(128)} %bitcast.core_ref, f32[256,128]{1,0:T(8,128)S(1)} %get-tuple-element.25.kept_ref, f32[256,128]{1,0:T(8,128)S(1)} %collective-permute-done.1.came_ref, bf16[768,128]{1,0:T(8,128)(2,1)S(1)} %copy-done.2, bf16[768,128]{1,0:T(8,128)(2,1)S(1)} %copy-done.3, ...), custom_call_target="tpu_custom_call" | custom-call | flops 2000000000 | bytes 4194304 | tf_op jit(solution)/shard_map/pallas_call | solution.py:315
  84.2 8.7 %all-to-all-done.2 = f32[32,24,128]{2,1,0:T(8,128)S(1)} async-done(((f32[32,24,128]{2,1,0:T(8,128)}), f32[32,24,128]{2,1,0:T(8,128)S(1)}, u32[]{:S(2)}, u32[]{:S(2)}) %all-to-all-start.2) | async-done | bytes 393248 | tf_op jit(solution)/shard_map/all_to_all | solution.py:311
  93.0 0.6 slice_bitcast_fusion
  (14 shorter events, 0.1 us)
Async XLA Ops:
  0.6 25.4 %copy-start.3 = (bf16[768,128]{1,0:T(8,128)(2,1)S(1)}, bf16[768,128]{1,0:T(8,128)(2,1)}, u32[]{:S(2)}) copy-start(bf16[768,128]{1,0:T(8,128)(2,1)} %read_ref.3) | copy-start | bytes 589828
  0.6 25.4 %copy-start.2 = (bf16[768,128]{1,0:T(8,128)(2,1)S(1)}, bf16[768,128]{1,0:T(8,128)(2,1)}, u32[]{:S(2)}) copy-start(bf16[768,128]{1,0:T(8,128)(2,1)} %write_ref.3) | copy-start | bytes 589828
  0.7 25.4 %copy-start.1 = (bf16[768,256]{1,0:T(8,128)(2,1)S(1)}, bf16[768,256]{1,0:T(8,128)(2,1)}, u32[]{:S(2)}) copy-start(bf16[768,256]{1,0:T(8,128)(2,1)} %g_ref.1) | copy-start | bytes 1179652
  0.7 25.4 %copy-start = (bf16[768,256]{1,0:T(8,128)(2,1)S(1)}, bf16[768,256]{1,0:T(8,128)(2,1)}, u32[]{:S(2)}) copy-start(bf16[768,256]{1,0:T(8,128)(2,1)} %x_ref.1) | copy-start | bytes 1179652
  4.3 34.2 %all-to-all-start = ((f32[32,17,1,128]{3,2,1,0:T(1,128)}), f32[32,17,1,128]{3,2,1,0:T(1,128)S(1)}, u32[]{:S(2)}, u32[]{:S(2)}) async-start(f32[32,17,1,128]{3,2,1,0:T(1,128)} %bitcast.15), calls=%async_computation | async-start | bytes 557056 | tf_op jit(solution)/shard_map/all_to_all | solution.py:276
  26.0 1.0 %copy-start.6 = (f32[768,24]{1,0:T(8,128)S(1)}, f32[768,24]{1,0:T(8,128)}, u32[]{:S(2)}) copy-start(f32[768,24]{1,0:T(8,128)} %get-tuple-element.20.cols_ref) | copy-start | bytes 221188
  27.0 0.7 copy-start.10
  35.3 1.0 %copy-start.4 = (f32[768,384]{1,0:T(8,128)}, f32[768,384]{1,0:T(8,128)S(1)}, u32[]{:S(2)}) copy-start(f32[768,384]{1,0:T(8,128)S(1)} %get-tuple-element.23.own_ref) | copy-start | bytes 3538948
  36.3 0.9 copy-start.8
  38.5 29.5 %copy-start.5 = (f32[768,384]{1,0:T(8,128)S(1)}, f32[768,384]{1,0:T(8,128)}, u32[]{:S(2)}) copy-start(f32[768,384]{1,0:T(8,128)} %copy-done.4) | copy-start | bytes 3538948
  38.6 29.4 %collective-permute-start = (f32[768,384]{1,0:T(8,128)S(1)}, f32[768,384]{1,0:T(8,128)S(1)}, u32[]{:S(2)}, u32[]{:S(2)}) collective-permute-start(f32[768,384]{1,0:T(8,128)S(1)} %get-tuple-element.24), channel_id=1, source_target_pairs={{0,1},{1,0},{2,3},{3,2},{4,5},{5,4},{6,7},{7,6},{8,9},{9,8},{10,11... | collective-permute-start | bytes 3538952 | tf_op jit(solution)/shard_map/ppermute | solution.py:303
  68.1 14.4 %copy-start.7 = (f32[768,24]{1,0:T(8,128)S(1)}, f32[768,24]{1,0:T(8,128)}, u32[]{:S(2)}) copy-start(f32[768,24]{1,0:T(8,128)} %get-tuple-element.20.cols_ref) | copy-start | bytes 221188
  68.1 14.4 %copy-start.9 = (f32[768,256]{1,0:T(8,128)S(1)}, f32[768,256]{1,0:T(8,128)}, u32[]{:S(2)}) copy-start(f32[768,256]{1,0:T(8,128)} %copy-done.8) | copy-start | bytes 2359300
  69.4 23.5 %all-to-all-start.2 = ((f32[32,24,128]{2,1,0:T(8,128)}), f32[32,24,128]{2,1,0:T(8,128)S(1)}, u32[]{:S(2)}, u32[]{:S(2)}) async-start(f32[32,24,128]{2,1,0:T(8,128)} %bitcast.5), calls=%async_computation.2 | async-start | bytes 786432 | tf_op jit(solution)/shard_map/all_to_all | solution.py:311
  79.2 3.2 %collective-permute-start.1 = (f32[256,128]{1,0:T(8,128)S(1)}, f32[256,128]{1,0:T(8,128)S(1)}, u32[]{:S(2)}, u32[]{:S(2)}) collective-permute-start(f32[256,128]{1,0:T(8,128)S(1)} %get-tuple-element.26), channel_id=1, source_target_pairs={{0,1},{1,0},{2,3},{3,2},{4,5},{5,4},{6,7},{7,6},{8,9},{9,8},{10,11... | collective-permute-start | bytes 393224 | tf_op jit(solution)/shard_map/ppermute | solution.py:314

commit v3 on v2

--- a/solution.py
+++ b/solution.py
@@ -42,7 +42,6 @@
     decay_hbm,
     send_ref,
     rows_ref,
-    cols_ref,
     x_ref,
     g_ref,
     write_ref,
@@ -90,10 +89,10 @@
         parts.append(inside + before)
         before = before + inside[:, lanes - 1 : lanes]
     cumul = jnp.concatenate(parts, axis=1)
-    rows_ref[...] = cumul
+    rows = jnp.concatenate([cumul, jnp.exp(cumul), jnp.exp(before - cumul)], axis=0)
+    rows_ref[...] = rows
     total = jnp.exp(before)
-    cols = jnp.concatenate([cumul, jnp.exp(cumul), jnp.exp(before - cumul)], axis=0).T
-    cols_ref[...] = cols
+    cols = rows.T
     per_head = head_size // chunk
     for flow, (values_ref, vectors_ref, column) in enumerate(
         ((x_ref, write_ref, 16), (g_ref, read_ref, 8))
@@ -119,7 +118,7 @@
                     send_ref[at : at + 1, :] = jnp.broadcast_to(total[head : head + 1], (1, width))
 
 
-def scan_kernel(sections, chunk, got_ref, cross_ref, out_ref, crossed_ref):
+def scan_kernel(sections, chunk, got_ref, after_ref, out_ref):
     stride = 2 * chunk + 1
 
     def total(section):
@@ -146,17 +145,38 @@
     write_ref,
     read_ref,
     rows_ref,
-    cols_ref,
+    y_hbm,
+    dx_hbm,
+    own_hbm,
+    cross_hbm,
+    after_ref,
     y_ref,
     dx_ref,
     own_ref,
     cross_ref,
     grad_ref,
+    left,
 ):
     tokens, channels = x_ref.shape
     head_size = channels // heads
     width = write_ref.shape[1]
     blocks = tokens // BLOCK
+    after_ref[0] = 0
+    started = []
+
+    def leave(source, target):
+        copy = pltpu.make_async_copy(source, target, left.at[len(started)])
+        copy.start()
+        started.append(copy)
+
+    first = core_ref[0] == 0
+    cols = rows_ref[...].T
+    x_weighted = x_ref[...].astype(f32) * lanes_of_heads(cols[:, 16:24], heads, head_size)
+    g_weighted = g_ref[...].astype(f32) * lanes_of_heads(cols[:, 8:16], heads, head_size)
+    own_ref[:, 0:channels] = jnp.where(first, x_weighted, g_weighted)
+    cross_ref[:, 0:channels] = jnp.where(first, g_weighted, x_weighted)
+    for source, target in ((own_ref, own_hbm), (cross_ref, cross_hbm)):
+        leave(source.at[:, pl.ds(0, channels)], target.at[:, pl.ds(0, channels)])
     y_ref[...] = jnp.zeros_like(y_ref)
     dx_ref[...] = jnp.zeros_like(dx_ref)
     grad_ref[...] = jnp.zeros_like(grad_ref)
@@ -175,7 +195,7 @@
             score_grad = jnp.zeros((BLOCK, BLOCK), f32)
             for head in range(heads):
                 own = slice(head * head_size, (head + 1) * head_size)
-                differ = cols_ref[t, head : head + 1] - rows_ref[head : head + 1, j]
+                differ = cols[t, head : head + 1] - rows_ref[head : head + 1, j]
                 if later == earlier:
                     differ = jnp.where(causal, differ, -jnp.inf)
                 decay = jnp.exp(differ)
@@ -185,42 +205,58 @@
                 y_ref[t, own] += dot(mixing, x_head, ((1,), (0,)))
                 dx_ref[j, own] += dot(mixing, g_head, ((0,), (0,)))
                 score_grad += dot(g_head, x_head, ((1,), (1,))) * decay
+            if later == blocks - 1:
+                at = pl.ds(earlier * BLOCK, BLOCK)
+                leave(dx_ref.at[at], dx_hbm.at[at])
             high, low = split(score_grad)
             grad_ref[j, 0:width] += dot(high, read, ((0,), (0,))) + dot(low, read, ((0,), (0,)))
             grad_ref[t, width:] += dot(high, write, ((1,), (0,))) + dot(low, write, ((1,), (0,)))
-    first = core_ref[0] == 0
+        at = pl.ds(later * BLOCK, BLOCK)
+        leave(y_ref.at[at], y_hbm.at[at])
     own_ref[:, channels:] = jnp.where(first, grad_ref[:, 0:width], grad_ref[:, width:])
     cross_ref[:, channels:] = jnp.where(first, grad_ref[:, width:], grad_ref[:, 0:width])
-    x_weighted = x_ref[...].astype(f32) * lanes_of_heads(cols_ref[:, 16:24], heads, head_size)
-    g_weighted = g_ref[...].astype(f32) * lanes_of_heads(cols_ref[:, 8:16], heads, head_size)
-    own_ref[:, 0:channels] = jnp.where(first, x_weighted, g_weighted)
-    cross_ref[:, 0:channels] = jnp.where(first, g_weighted, x_weighted)
-
-
-def carry_kernel(core_ref, state_ref, own_ref, other_ref, out_ref, kept_ref, swap_ref):
+    for source, target in ((own_ref, own_hbm), (cross_ref, cross_hbm)):
+        leave(source.at[:, pl.ds(channels, width)], target.at[:, pl.ds(channels, width)])
+    for copy in started:
+        copy.wait()
+
+
+def carry_kernel(
+    core_ref, state_ref, came_ref, own_hbm, other_hbm, out_ref, own_ref, other_ref, arrived
+):
+    blocks = own_ref.shape[0] // BLOCK
+    copies = []
+    for block in range(blocks):
+        at = pl.ds(block * BLOCK, BLOCK)
+        for flow, (source, target) in enumerate(((own_hbm, own_ref), (other_hbm, other_ref))):
+            copy = pltpu.make_async_copy(source.at[at], target.at[at], arrived.at[block, flow])
+            copy.start()
+            copies.append(copy)
     core = core_ref[0]
-    channels = own_ref.shape[1] - out_ref.shape[1]
     width = out_ref.shape[1]
-    flat = (channels, width)
-    mine = state_ref[:, pl.ds(core, 1)].reshape(flat)
-    partner = state_ref[:, pl.ds(1 - core, 1)].reshape(flat)
-    kept_ref[...] = mine
-    swap_ref[...] = partner
-    total = own_ref[:, channels:] + other_ref[:, channels:]
-    for values_ref, state in ((own_ref, mine), (other_ref, partner)):
-        high, low = split(values_ref[:, 0:channels])
-        state_high, state_low = split(state)
-        product = dot(high, jnp.concatenate([state_high, state_low], axis=1), ((1,), (0,)))
-        total += product[:, :width] + product[:, width:] + dot(low, state_high, ((1,), (0,)))
-    out_ref[...] = total
+    channels = own_ref.shape[1] - width
+    factors = []
+    for states_ref in (state_ref, came_ref):
+        high, low = split(states_ref[:, pl.ds(core, 1)].reshape(channels, width))
+        factors.append((jnp.concatenate([high, low], axis=1), high))
+    for block in range(blocks):
+        t = slice(block * BLOCK, (block + 1) * BLOCK)
+        copies[2 * block].wait()
+        copies[2 * block + 1].wait()
+        total = own_ref[t, channels:] + other_ref[t, channels:]
+        for values_ref, (both, first) in zip((own_ref, other_ref), factors):
+            high, low = split(values_ref[t, 0:channels])
+            product = dot(high, both, ((1,), (0,)))
+            total += product[:, :width] + product[:, width:] + dot(low, first, ((1,), (0,)))
+        out_ref[t, :] = total
 
 
 def finish_kernel(
-    heads, core_ref, kept_ref, came_ref, write_ref, read_ref, cols_ref, y_ref, dx_ref, out_ref, dout_ref
+    heads, state_ref, write_ref, read_ref, rows_ref, y_ref, dx_ref, out_ref, dout_ref
 ):
-    first = core_ref[0] == 0
-    forward = jnp.where(first, came_ref[...], kept_ref[...])
-    backward = jnp.where(first, kept_ref[...], came_ref[...])
+    channels, width = out_ref.shape[1], write_ref.shape[1]
+    backward = state_ref[:, 0].reshape(channels, width)
+    forward = state_ref[:, 1].reshape(channels, width)
     head_size = forward.shape[0] // heads
     read, write = read_ref[...], write_ref[...]
 
@@ -231,20 +267,24 @@
             ((1,), (1,)),
         )
 
-    lead = lanes_of_heads(cols_ref[:, 8:16], heads, head_size)
+    cols = rows_ref[...].T
+    lead = lanes_of_heads(cols[:, 8:16], heads, head_size)
     out_ref[...] = (y_ref[...] + inter(read, forward) * lead).astype(bf16)
-    tail = lanes_of_heads(cols_ref[:, 16:24], heads, head_size)
+    tail = lanes_of_heads(cols[:, 16:24], heads, head_size)
     dout_ref[...] = (dx_ref[...] + inter(write, backward) * tail).astype(bf16)
 
 
-def call(kernel, outs, specs, cost, mebibytes, scratch=(), out_specs=None, **more):
+def in_hbm(value):
+    return pltpu.with_memory_space_constraint(value, pltpu.HBM)
+
+
+def call(kernel, outs, specs, cost, mebibytes, out_specs=None, **more):
     return pl.pallas_call(
         kernel,
         out_shape=[jax.ShapeDtypeStruct(shape, dtype) for shape, dtype in outs],
         in_specs=specs,
         out_specs=out_specs or [VMEM] * len(outs),
-        scratch_shapes=list(scratch),
-        compiler_params=pltpu.CompilerParams(vmem_limit_bytes=mebibytes * 2**20),
+        compiler_params=pltpu.CompilerParams(vmem_limit_bytes=int(mebibytes * 2**20)),
         cost_estimate=pl.CostEstimate(flops=cost, bytes_accessed=4 * 2**20, transcendentals=0),
         **more,
     )
@@ -258,13 +298,14 @@
     stride = 2 * chunk + 1
     core = lax.axis_index("core").reshape(1)
     swap_cores = [(0, 1), (1, 0)]
-    send, rows, cols = call(
+    wide = channels + width
+    send, rows = call(
         functools.partial(local_kernel, sections),
-        [((sections * stride, width), f32), ((8, tokens), f32), ((tokens, 24), f32)],
+        [((sections * stride, width), f32), ((24, tokens), f32)],
         [ANY] * 5,
         10**9,
-        60,
-        [
+        16,
+        scratch_shapes=[
             pltpu.VMEM(inputs.shape, bf16),
             pltpu.VMEM(inputs.shape, bf16),
             pltpu.VMEM(write_proj.shape, bf16),
@@ -272,53 +313,63 @@
             pltpu.VMEM(log_decay.shape, f32),
             pltpu.SemaphoreType.DMA((5,)),
         ],
-    )(inputs, grad_out, write_proj, read_proj, log_decay)
+    )(*(in_hbm(value) for value in (inputs, grad_out, write_proj, read_proj, log_decay)))
     got = lax.all_to_all(send.reshape(sections, stride, 1, width), ("x", "zh"), 0, 0)
     got = got.reshape(sections * stride, width)
-    y_intra, dx_intra, own, cross = call(
+    y_intra, dx_intra, own, cross, after = call(
         functools.partial(intra_kernel, heads),
         [
             ((tokens, channels), f32),
             ((tokens, channels), f32),
-            ((tokens, channels + width), f32),
-            ((tokens, channels + width), f32),
+            ((tokens, wide), f32),
+            ((tokens, wide), f32),
+            ((1,), jnp.int32),
         ],
-        [SMEM] + [VMEM] * 6,
+        [SMEM] + [VMEM] * 5,
         8 * 10**9,
-        16,
-        [pltpu.VMEM((tokens, 2 * width), f32)],
-    )(core, inputs, grad_out, write_proj, read_proj, rows, cols)
-    states, cross = call(
+        52.0,
+        out_specs=[ANY] * 4 + [SMEM],
+        scratch_shapes=[
+            pltpu.VMEM((tokens, channels), f32),
+            pltpu.VMEM((tokens, channels), f32),
+            pltpu.VMEM((tokens, wide), f32),
+            pltpu.VMEM((tokens, wide), f32),
+            pltpu.VMEM((tokens, 2 * width), f32),
+            pltpu.SemaphoreType.DMA((2 * (tokens // BLOCK) + 4,)),
+        ],
+    )(core, inputs, grad_out, write_proj, read_proj, rows)
+    (states,) = call(
         functools.partial(scan_kernel, sections, chunk),
-        [((sections, 2, chunk, width), f32), (cross.shape, f32)],
-        [VMEM, ANY],
+        [((sections, 2, chunk, width), f32)],
+        [VMEM, SMEM],
         10**8,
-        4,
-        out_specs=[VMEM, ANY],
-        input_output_aliases={1: 1},
-    )(got, cross)
-    mine = lax.all_to_all(
-        states.reshape(2 * sections, chunk, width), ("x", "zh", "core"), 0, 0
-    ).reshape(sections, 2, chunk, width)
+        4.0,
+    )(got, after)
+    mine = lax.all_to_all(states, ("x", "zh"), 0, 0)
     other = lax.ppermute(cross, "core", swap_cores)
-    piece, kept, swap = call(
+    came = lax.ppermute(mine, "core", swap_cores)
+    (piece,) = call(
         carry_kernel,
-        [((tokens, width), f32), ((channels, width), f32), ((channels, width), f32)],
-        [SMEM] + [VMEM] * 3,
+        [((tokens, width), f32)],
+        [SMEM, VMEM, VMEM, ANY, ANY],
         10**9,
-        12,
-    )(core, mine, own, other)
+        16.0,
+        scratch_shapes=[
+            pltpu.VMEM((tokens, wide), f32),
+            pltpu.VMEM((tokens, wide), f32),
+            pltpu.SemaphoreType.DMA((tokens // BLOCK, 2)),
+        ],
+    )(core, mine, came, in_hbm(own), other)
     parts = lax.all_to_all(
         piece.reshape(2 * spread, tokens // (2 * spread), width), ("y", "zl", "core"), 0, 0
     )
-    came = lax.ppermute(swap, "core", swap_cores)
     outputs, grad_inputs = call(
         functools.partial(finish_kernel, heads),
         [((tokens, channels), bf16)] * 2,
-        [SMEM] + [VMEM] * 7,
+        [VMEM] * 6,
         2 * 10**9,
-        12,
-    )(core, kept, came, write_proj, read_proj, cols, y_intra, dx_intra)
+        12.0,
+    )(mine, write_proj, read_proj, rows, y_intra, dx_intra)
     summed = jnp.sum(parts.reshape(spread, 2, -1, width), axis=0)
     return (outputs, grad_inputs, summed[0], summed[1])
 

time: 94.1 us -> 97.2 us (1.033)
  the two profiles are of different devices: /device:TPU:1 before, /device:TPU:2 now
where the time goes in v3:
time: 97.2 us; the launch traced here: 96.8 us
  starting transfers between devices  35 us (36%)
  blocking collectives  23.6 us (24%)
  Pallas kernels  18.5 us (19%)
  waiting for transfers between devices  18.3 us (19%)
    all_to_all x1, blocking collectives, per_device(): mine = lax.all_to_all(states, ('x', 'zh'), 0, 0)  23.6 us
    all_to_all x1, starting transfers between devices, per_device(): lax.all_to_all(send.reshape(sections, stride, 1, width), ('x', 'zh'), 0, 0)  21.4 us
    all_to_all x1, waiting for transfers between devices, per_device(): lax.all_to_all(piece.reshape(2 * spread, tokens // (2 * spread), width),...  13.2 us
    all_to_all x1, starting transfers between devices, per_device(): lax.all_to_all(piece.reshape(2 * spread, tokens // (2 * spread), width),...  9.76 us
    pallas_call x1, Pallas kernels, per_device(): call(functools.partial(intra_kernel, heads), [((tokens, channels), f32),...  9.3 us
    pallas_call x1, Pallas kernels, per_device(): call(functools.partial(local_kernel, sections), [((sections * stride, wid...  3.66 us
    all_to_all x1, waiting for transfers between devices, per_device(): lax.all_to_all(send.reshape(sections, stride, 1, width), ('x', 'zh'), 0, 0)  3.56 us
    pallas_call x1, Pallas kernels, per_device(): call(carry_kernel, [((tokens, width), f32)], [SMEM, VMEM, VMEM, ANY, ANY]...  2.86 us
  transfers between devices with their start and end apart: 4, of which 3 were waited for; matrix products, arithmetic and copies ran while one was open for 0% of the time, Pallas kernels for 12%

profile of v3, /device:TPU:2, one launch (start us, length us, event | category | flops | bytes accessed | tf_op | source)
XLA Modules:
  0.0 96.8 jit_solution(7326392184346143370)
XLA Ops:
  0.6 0.0 copy-start.3
  0.6 0.0 copy-start.2
  0.7 0.0 copy-start.1
  0.7 0.0 copy-start
  0.7 3.7 %shard_map.84 = (f32[544,128]{1,0:T(8,128)}, f32[24,768]{1,0:T(8,128)S(1)}) custom-call(bf16[768,256]{1,0:T(8,128)(2,1)} %x_ref.1, bf16[768,256]{1,0:T(8,128)(2,1)} %g_ref.1, bf16[768,128]{1,0:T(8,128)(2,1)} %write_ref.3, bf16[768,128]{1,0:T(8,128)(2,1)} %read_ref.3, f32[4,768]{1,0:T(4,128)} %decay_hbm.1), custom_call_target="tpu_custom_call" | custom-call | flops 1000000000 | bytes 4194304 | tf_op jit(solution)/shard_map/pallas_call | solution.py:302
  4.3 21.4 %all-to-all-start = ((f32[32,17,1,128]{3,2,1,0:T(1,128)}), f32[32,17,1,128]{3,2,1,0:T(1,128)S(1)}, u32[]{:S(2)}, u32[]{:S(2)}) async-start(f32[32,17,1,128]{3,2,1,0:T(1,128)} %bitcast), calls=%async_computation | async-start | bytes 557056 | tf_op jit(solution)/shard_map/all_to_all | solution.py:317
  25.7 0.0 copy-done.3
  25.8 0.0 copy-done.2
  25.8 0.0 copy-done.1
  25.8 0.0 copy-done
  25.8 9.3 %shard_map.85 = (f32[768,256]{1,0:T(8,128)}, f32[768,256]{1,0:T(8,128)}, f32[768,384]{1,0:T(8,128)}, f32[768,384]{1,0:T(8,128)}, s32[1]{0:T(128)}) custom-call(s32[1]{0:T(128)} %bitcast.2.core_ref, bf16[768,256]{1,0:T(8,128)(2,1)S(1)} %copy-done, bf16[768,256]{1,0:T(8,128)(2,1)S(1)} %copy-done.1, bf16[768,128]{1,0:T(8,128)(2,1)S(1)} %copy-done.2, ...), custom_call_target="tpu_custom_call" | custom-call | flops 8000000000 | bytes 4194304 | tf_op jit(solution)/shard_map/pallas_call | solution.py:319
  35.1 1.9 %collective-permute-start.1 = (f32[768,384]{1,0:T(8,128)}, f32[768,384]{1,0:T(8,128)S(1)}, u32[]{:S(2)}, u32[]{:S(2)}) collective-permute-start(f32[768,384]{1,0:T(8,128)} %get-tuple-element.21), channel_id=1, source_target_pairs={{0,1},{1,0},{2,3},{3,2},{4,5},{5,4},{6,7},{7,6},{8,9},{9,8},{10,11... | collective-permute-start | bytes 3538952 | tf_op jit(solution)/shard_map/ppermute | solution.py:349
  37.0 3.6 %all-to-all-done = f32[32,17,1,128]{3,2,1,0:T(1,128)S(1)} async-done(((f32[32,17,1,128]{3,2,1,0:T(1,128)}), f32[32,17,1,128]{3,2,1,0:T(1,128)S(1)}, u32[]{:S(2)}, u32[]{:S(2)}) %all-to-all-start) | async-done | bytes 278560 | tf_op jit(solution)/shard_map/all_to_all | solution.py:317
  40.6 0.7 shard_map.86
  41.3 23.6 %all_to_all.15.state_ref = f32[32,2,8,128]{3,2,1,0:T(8,128)S(1)} all-to-all(f32[32,2,8,128]{3,2,1,0:T(8,128)S(1)} %shard_map.86), channel_id=1, replica_groups=mesh['x'=8,'zh'=4,'y'=8,'zl'=2,'core'=2] {'x','zh'}, dimensions={0} | all-to-all | bytes 524288 | tf_op jit(solution)/shard_map/all_to_all | solution.py:348
  64.9 1.9 %collective-permute-start = (f32[32,2,8,128]{3,2,1,0:T(8,128)S(1)}, f32[32,2,8,128]{3,2,1,0:T(8,128)S(1)}, u32[]{:S(2)}, u32[]{:S(2)}) collective-permute-start(f32[32,2,8,128]{3,2,1,0:T(8,128)S(1)} %all_to_all.15.state_ref), channel_id=1, source_target_pairs={{0,1},{1,0},{2,3},{3,2},{4,5},{5,4},{6,7},{7,6},{8,9},{9,8},{10,11... | collective-permute-start | bytes 786440 | tf_op jit(solution)/shard_map/ppermute | solution.py:350
  66.8 0.0 collective-permute-done.1.other_hbm
  66.8 1.5 %collective-permute-done.came_ref = f32[32,2,8,128]{3,2,1,0:T(8,128)S(1)} collective-permute-done((f32[32,2,8,128]{3,2,1,0:T(8,128)S(1)}, f32[32,2,8,128]{3,2,1,0:T(8,128)S(1)}, u32[]{:S(2)}, u32[]{:S(2)}) %collective-permute-start) | collective-permute-done | bytes 262176 | tf_op jit(solution)/shard_map/ppermute | solution.py:350
  68.3 2.9 %shard_map.88 = f32[768,128]{1,0:T(8,128)} custom-call(s32[1]{0:T(128)} %bitcast.2.core_ref, f32[32,2,8,128]{3,2,1,0:T(8,128)S(1)} %all_to_all.15.state_ref, f32[32,2,8,128]{3,2,1,0:T(8,128)S(1)} %collective-permute-done.came_ref, f32[768,384]{1,0:T(8,128)} %get-tuple-element.20.own_hbm, f32[768,384]{1,0:T(8,128)S(1)} %collective-permute-done.1.other_hbm), custom_call_target="tpu_custom_call" | custom-call | flops 1000000000 | bytes 4194304 | tf_op jit(solution)/shard_map/pallas_call | solution.py:351
  71.2 9.8 %all-to-all-start.2 = ((f32[32,24,128]{2,1,0:T(8,128)}), f32[32,24,128]{2,1,0:T(8,128)S(1)}, u32[]{:S(2)}, u32[]{:S(2)}) async-start(f32[32,24,128]{2,1,0:T(8,128)} %bitcast.3), calls=%async_computation.2 | async-start | bytes 786432 | tf_op jit(solution)/shard_map/all_to_all | solution.py:363
  80.9 0.0 copy-done.4
  81.0 1.9 %shard_map.87 = (bf16[768,256]{1,0:T(8,128)(2,1)}, bf16[768,256]{1,0:T(8,128)(2,1)}) custom-call(f32[32,2,8,128]{3,2,1,0:T(8,128)S(1)} %all_to_all.15.state_ref, bf16[768,128]{1,0:T(8,128)(2,1)S(1)} %copy-done.2, bf16[768,128]{1,0:T(8,128)(2,1)S(1)} %copy-done.3, f32[24,768]{1,0:T(8,128)S(1)} %get-tuple-element.14.rows_ref, f32[768,256]{1,0:T(8,128)S(1)} %copy-done.4, ...), custom_call_target="tpu_custom_call" | custom-call | flops 2000000000 | bytes 4194304 | tf_op jit(solution)/shard_map/pallas_call | solution.py:366
  82.9 13.2 %all-to-all-done.2 = f32[32,24,128]{2,1,0:T(8,128)S(1)} async-done(((f32[32,24,128]{2,1,0:T(8,128)}), f32[32,24,128]{2,1,0:T(8,128)S(1)}, u32[]{:S(2)}, u32[]{:S(2)}) %all-to-all-start.2) | async-done | bytes 393248 | tf_op jit(solution)/shard_map/all_to_all | solution.py:363
  96.2 0.6 slice_bitcast_fusion
  (4 shorter events, 0.0 us)
Async XLA Ops:
  0.6 25.1 %copy-start.3 = (bf16[768,128]{1,0:T(8,128)(2,1)S(1)}, bf16[768,128]{1,0:T(8,128)(2,1)}, u32[]{:S(2)}) copy-start(bf16[768,128]{1,0:T(8,128)(2,1)} %read_ref.3) | copy-start | bytes 589828
  0.6 25.1 %copy-start.2 = (bf16[768,128]{1,0:T(8,128)(2,1)S(1)}, bf16[768,128]{1,0:T(8,128)(2,1)}, u32[]{:S(2)}) copy-start(bf16[768,128]{1,0:T(8,128)(2,1)} %write_ref.3) | copy-start | bytes 589828
  0.7 25.1 %copy-start.1 = (bf16[768,256]{1,0:T(8,128)(2,1)S(1)}, bf16[768,256]{1,0:T(8,128)(2,1)}, u32[]{:S(2)}) copy-start(bf16[768,256]{1,0:T(8,128)(2,1)} %g_ref.1) | copy-start | bytes 1179652
  0.7 25.1 %copy-start = (bf16[768,256]{1,0:T(8,128)(2,1)S(1)}, bf16[768,256]{1,0:T(8,128)(2,1)}, u32[]{:S(2)}) copy-start(bf16[768,256]{1,0:T(8,128)(2,1)} %x_ref.1) | copy-start | bytes 1179652
  4.3 36.2 %all-to-all-start = ((f32[32,17,1,128]{3,2,1,0:T(1,128)}), f32[32,17,1,128]{3,2,1,0:T(1,128)S(1)}, u32[]{:S(2)}, u32[]{:S(2)}) async-start(f32[32,17,1,128]{3,2,1,0:T(1,128)} %bitcast), calls=%async_computation | async-start | bytes 557056 | tf_op jit(solution)/shard_map/all_to_all | solution.py:317
  35.1 31.7 %collective-permute-start.1 = (f32[768,384]{1,0:T(8,128)}, f32[768,384]{1,0:T(8,128)S(1)}, u32[]{:S(2)}, u32[]{:S(2)}) collective-permute-start(f32[768,384]{1,0:T(8,128)} %get-tuple-element.21), channel_id=1, source_target_pairs={{0,1},{1,0},{2,3},{3,2},{4,5},{5,4},{6,7},{7,6},{8,9},{9,8},{10,11... | collective-permute-start | bytes 3538952 | tf_op jit(solution)/shard_map/ppermute | solution.py:349
  64.9 3.4 %collective-permute-start = (f32[32,2,8,128]{3,2,1,0:T(8,128)S(1)}, f32[32,2,8,128]{3,2,1,0:T(8,128)S(1)}, u32[]{:S(2)}, u32[]{:S(2)}) collective-permute-start(f32[32,2,8,128]{3,2,1,0:T(8,128)S(1)} %all_to_all.15.state_ref), channel_id=1, source_target_pairs={{0,1},{1,0},{2,3},{3,2},{4,5},{5,4},{6,7},{7,6},{8,9},{9,8},{10,11... | collective-permute-start | bytes 786440 | tf_op jit(solution)/shard_map/ppermute | solution.py:350
  68.3 12.6 %copy-start.4 = (f32[768,256]{1,0:T(8,128)S(1)}, f32[768,256]{1,0:T(8,128)}, u32[]{:S(2)}) copy-start(f32[768,256]{1,0:T(8,128)} %get-tuple-element.16.y_ref) | copy-start | bytes 2359300
  68.3 12.7 %copy-start.5 = (f32[768,256]{1,0:T(8,128)S(1)}, f32[768,256]{1,0:T(8,128)}, u32[]{:S(2)}) copy-start(f32[768,256]{1,0:T(8,128)} %get-tuple-element.17.dx_ref) | copy-start | bytes 2359300
  71.2 25.0 %all-to-all-start.2 = ((f32[32,24,128]{2,1,0:T(8,128)}), f32[32,24,128]{2,1,0:T(8,128)S(1)}, u32[]{:S(2)}, u32[]{:S(2)}) async-start(f32[32,24,128]{2,1,0:T(8,128)} %bitcast.3), calls=%async_computation.2 | async-start | bytes 786432 | tf_op jit(solution)/shard_map/all_to_all | solution.py:363

commit v4 on v3

--- a/solution.py
+++ b/solution.py
@@ -118,7 +118,7 @@
                     send_ref[at : at + 1, :] = jnp.broadcast_to(total[head : head + 1], (1, width))
 
 
-def scan_kernel(sections, chunk, got_ref, after_ref, out_ref):
+def scan_kernel(sections, chunk, got_ref, out_ref):
     stride = 2 * chunk + 1
 
     def total(section):
@@ -128,18 +128,18 @@
     running = jnp.zeros((chunk, got_ref.shape[1]), f32)
     for section in range(sections):
         base = section * stride
-        out_ref[section, 1] = running
+        out_ref[section, 0:chunk, :] = running
         running = total(section) * running + got_ref[base : base + chunk, :]
     running = jnp.zeros((chunk, got_ref.shape[1]), f32)
     for section in range(sections - 1, -1, -1):
         base = section * stride + chunk
-        out_ref[section, 0] = running
+        out_ref[section, chunk : 2 * chunk, :] = running
         running = total(section) * running + got_ref[base : base + chunk, :]
 
 
 def intra_kernel(
     heads,
-    core_ref,
+    laters,
     x_ref,
     g_ref,
     write_ref,
@@ -147,44 +147,33 @@
     rows_ref,
     y_hbm,
     dx_hbm,
-    own_hbm,
-    cross_hbm,
-    after_ref,
+    grad_hbm,
     y_ref,
     dx_ref,
-    own_ref,
-    cross_ref,
     grad_ref,
     left,
 ):
-    tokens, channels = x_ref.shape
+    channels = x_ref.shape[1]
     head_size = channels // heads
     width = write_ref.shape[1]
-    blocks = tokens // BLOCK
-    after_ref[0] = 0
     started = []
 
-    def leave(source, target):
-        copy = pltpu.make_async_copy(source, target, left.at[len(started)])
+    def leave(source, target, first, count):
+        at = pl.ds(first, count)
+        copy = pltpu.make_async_copy(source.at[at], target.at[at], left.at[len(started)])
         copy.start()
         started.append(copy)
 
-    first = core_ref[0] == 0
     cols = rows_ref[...].T
-    x_weighted = x_ref[...].astype(f32) * lanes_of_heads(cols[:, 16:24], heads, head_size)
-    g_weighted = g_ref[...].astype(f32) * lanes_of_heads(cols[:, 8:16], heads, head_size)
-    own_ref[:, 0:channels] = jnp.where(first, x_weighted, g_weighted)
-    cross_ref[:, 0:channels] = jnp.where(first, g_weighted, x_weighted)
-    for source, target in ((own_ref, own_hbm), (cross_ref, cross_hbm)):
-        leave(source.at[:, pl.ds(0, channels)], target.at[:, pl.ds(0, channels)])
     y_ref[...] = jnp.zeros_like(y_ref)
     dx_ref[...] = jnp.zeros_like(dx_ref)
     grad_ref[...] = jnp.zeros_like(grad_ref)
     causal = lax.broadcasted_iota(jnp.int32, (BLOCK, BLOCK), 0) >= lax.broadcasted_iota(
         jnp.int32, (BLOCK, BLOCK), 1
     )
-    for later in range(blocks):
+    for place, later in enumerate(laters):
         t = slice(later * BLOCK, (later + 1) * BLOCK)
+        mine = slice(place * BLOCK, (place + 1) * BLOCK)
         read = read_ref[t, :]
         g_block = g_ref[t, :]
         for earlier in range(later + 1):
@@ -202,61 +191,104 @@
                 mixing = (scores * decay).astype(bf16)
                 x_head = x_block[:, own]
                 g_head = g_block[:, own]
-                y_ref[t, own] += dot(mixing, x_head, ((1,), (0,)))
+                y_ref[mine, own] += dot(mixing, x_head, ((1,), (0,)))
                 dx_ref[j, own] += dot(mixing, g_head, ((0,), (0,)))
                 score_grad += dot(g_head, x_head, ((1,), (1,))) * decay
-            if later == blocks - 1:
-                at = pl.ds(earlier * BLOCK, BLOCK)
-                leave(dx_ref.at[at], dx_hbm.at[at])
             high, low = split(score_grad)
             grad_ref[j, 0:width] += dot(high, read, ((0,), (0,))) + dot(low, read, ((0,), (0,)))
             grad_ref[t, width:] += dot(high, write, ((1,), (0,))) + dot(low, write, ((1,), (0,)))
-        at = pl.ds(later * BLOCK, BLOCK)
-        leave(y_ref.at[at], y_hbm.at[at])
-    own_ref[:, channels:] = jnp.where(first, grad_ref[:, 0:width], grad_ref[:, width:])
-    cross_ref[:, channels:] = jnp.where(first, grad_ref[:, width:], grad_ref[:, 0:width])
-    for source, target in ((own_ref, own_hbm), (cross_ref, cross_hbm)):
-        leave(source.at[:, pl.ds(channels, width)], target.at[:, pl.ds(channels, width)])
+            if place == len(laters) - 1:
+                leave(dx_ref, dx_hbm, earlier * BLOCK, BLOCK)
+                if earlier < later:
+                    leave(grad_ref, grad_hbm, earlier * BLOCK, BLOCK)
+        leave(y_ref, y_hbm, place * BLOCK, BLOCK)
+    leave(grad_ref, grad_hbm, laters[-1] * BLOCK, BLOCK)
     for copy in started:
         copy.wait()
 
 
+def states_of(state_ref, chunk):
+    forward = state_ref[:, 0:chunk, :]
+    backward = state_ref[:, chunk:, :]
+    flat = (forward.shape[0] * chunk, forward.shape[2])
+    return forward.reshape(flat), backward.reshape(flat)
+
+
+def carried(values, state, columns, heads):
+    rows, width = state.shape
+    row_head = lax.broadcasted_iota(jnp.int32, (rows, 1), 0) // (rows // heads)
+    total = None
+    for head in range(heads):
+        mine = jnp.where(row_head == head, state, 0.0)
+        product = dot(values, jnp.concatenate(split(mine), axis=1), ((1,), (0,)))
+        product = (product[:, :width] + product[:, width:]) * columns[:, head : head + 1]
+        total = product if total is None else total + product
+    return total
+
+
 def carry_kernel(
-    core_ref, state_ref, came_ref, own_hbm, other_hbm, out_ref, own_ref, other_ref, arrived
+    heads,
+    chunk,
+    group,
+    core_ref,
+    state_ref,
+    x_ref,
+    g_ref,
+    rows_ref,
+    late_hbm,
+    early_hbm,
+    keep_ref,
+    send_ref,
+    late_ref,
+    early_ref,
+    arrived,
 ):
-    blocks = own_ref.shape[0] // BLOCK
-    copies = []
-    for block in range(blocks):
-        at = pl.ds(block * BLOCK, BLOCK)
-        for flow, (source, target) in enumerate(((own_hbm, own_ref), (other_hbm, other_ref))):
-            copy = pltpu.make_async_copy(source.at[at], target.at[at], arrived.at[block, flow])
-            copy.start()
-            copies.append(copy)
-    core = core_ref[0]
-    width = out_ref.shape[1]
-    channels = own_ref.shape[1] - width
-    factors = []
-    for states_ref in (state_ref, came_ref):
-        high, low = split(states_ref[:, pl.ds(core, 1)].reshape(channels, width))
-        factors.append((jnp.concatenate([high, low], axis=1), high))
-    for block in range(blocks):
-        t = slice(block * BLOCK, (block + 1) * BLOCK)
-        copies[2 * block].wait()
-        copies[2 * block + 1].wait()
-        total = own_ref[t, channels:] + other_ref[t, channels:]
-        for values_ref, (both, first) in zip((own_ref, other_ref), factors):
-            high, low = split(values_ref[t, 0:channels])
-            product = dot(high, both, ((1,), (0,)))
-            total += product[:, :width] + product[:, width:] + dot(low, first, ((1,), (0,)))
-        out_ref[t, :] = total
+    copies = [
+        pltpu.make_async_copy(late_hbm, late_ref, arrived.at[0]),
+        pltpu.make_async_copy(early_hbm, early_ref, arrived.at[1]),
+    ]
+    for copy in copies:
+        copy.start()
+    forward, backward = states_of(state_ref, chunk)
+    width = forward.shape[1]
+    count = keep_ref.shape[0]
+    cols = rows_ref[...].T
+    of_write = carried(x_ref[...], backward, cols[:, 16:24], heads)
+    of_read = carried(g_ref[...], forward, cols[:, 8:16], heads)
+    for copy in copies:
+        copy.wait()
+    known = early_ref.shape[0]
+    late = late_ref[...]
+    intra = jnp.concatenate([late[:known] + early_ref[...], late[known:]], axis=0)
+    whole = jnp.concatenate([of_write, of_read], axis=1) + intra
+    whole = whole.reshape(count, 2, group, 2 * width)
+
+    @pl.when(core_ref[0] == 0)
+    def _():
+        keep_ref[...] = whole[:, 0]
+        send_ref[...] = whole[:, 1]
+
+    @pl.when(core_ref[0] != 0)
+    def _():
+        keep_ref[...] = whole[:, 1]
+        send_ref[...] = whole[:, 0]
 
 
 def finish_kernel(
-    heads, state_ref, write_ref, read_ref, rows_ref, y_ref, dx_ref, out_ref, dout_ref
+    heads,
+    chunk,
+    state_ref,
+    write_ref,
+    read_ref,
+    rows_ref,
+    y_late_ref,
+    y_early_ref,
+    dx_late_ref,
+    dx_early_ref,
+    out_ref,
+    dout_ref,
 ):
-    channels, width = out_ref.shape[1], write_ref.shape[1]
-    backward = state_ref[:, 0].reshape(channels, width)
-    forward = state_ref[:, 1].reshape(channels, width)
+    forward, backward = states_of(state_ref, chunk)
     head_size = forward.shape[0] // heads
     read, write = read_ref[...], write_ref[...]
 
@@ -267,11 +299,14 @@
             ((1,), (1,)),
         )
 
+    known = y_early_ref.shape[0]
     cols = rows_ref[...].T
-    lead = lanes_of_heads(cols[:, 8:16], heads, head_size)
-    out_ref[...] = (y_ref[...] + inter(read, forward) * lead).astype(bf16)
-    tail = lanes_of_heads(cols[:, 16:24], heads, head_size)
-    dout_ref[...] = (dx_ref[...] + inter(write, backward) * tail).astype(bf16)
+    outer = inter(read, forward) * lanes_of_heads(cols[:, 8:16], heads, head_size)
+    out_ref[0:known, :] = (y_early_ref[...] + outer[:known]).astype(bf16)
+    out_ref[known:, :] = (y_late_ref[...] + outer[known:]).astype(bf16)
+    outer = inter(write, backward) * lanes_of_heads(cols[:, 16:24], heads, head_size)
+    dout_ref[0:known, :] = (dx_late_ref[0:known, :] + dx_early_ref[...] + outer[:known]).astype(bf16)
+    dout_ref[known:, :] = (dx_late_ref[known:, :] + outer[known:]).astype(bf16)
 
 
 def in_hbm(value):
@@ -298,7 +333,6 @@
     stride = 2 * chunk + 1
     core = lax.axis_index("core").reshape(1)
     swap_cores = [(0, 1), (1, 0)]
-    wide = channels + width
     send, rows = call(
         functools.partial(local_kernel, sections),
         [((sections * stride, width), f32), ((24, tokens), f32)],
@@ -316,62 +350,61 @@
     )(*(in_hbm(value) for value in (inputs, grad_out, write_proj, read_proj, log_decay)))
     got = lax.all_to_all(send.reshape(sections, stride, 1, width), ("x", "zh"), 0, 0)
     got = got.reshape(sections * stride, width)
-    y_intra, dx_intra, own, cross, after = call(
-        functools.partial(intra_kernel, heads),
-        [
-            ((tokens, channels), f32),
-            ((tokens, channels), f32),
-            ((tokens, wide), f32),
-            ((tokens, wide), f32),
-            ((1,), jnp.int32),
-        ],
-        [SMEM] + [VMEM] * 5,
-        8 * 10**9,
-        52.0,
-        out_specs=[ANY] * 4 + [SMEM],
-        scratch_shapes=[
-            pltpu.VMEM((tokens, channels), f32),
-            pltpu.VMEM((tokens, channels), f32),
-            pltpu.VMEM((tokens, wide), f32),
-            pltpu.VMEM((tokens, wide), f32),
-            pltpu.VMEM((tokens, 2 * width), f32),
-            pltpu.SemaphoreType.DMA((2 * (tokens // BLOCK) + 4,)),
-        ],
-    )(core, inputs, grad_out, write_proj, read_proj, rows)
+
+    def intra(laters):
+        sizes = (
+            (len(laters) * BLOCK, channels),
+            ((laters[-1] + 1) * BLOCK, channels),
+            ((laters[-1] + 1) * BLOCK, 2 * width),
+        )
+        parts = call(
+            functools.partial(intra_kernel, heads, laters),
+            [(size, f32) for size in sizes],
+            [VMEM] * 5,
+            4 * 10**9,
+            52,
+            out_specs=[ANY] * 3,
+            scratch_shapes=[
+                *(pltpu.VMEM(size, f32) for size in sizes),
+                pltpu.SemaphoreType.DMA((len(laters) + 2 * (laters[-1] + 1),)),
+            ],
+        )(inputs, grad_out, write_proj, read_proj, rows)
+        return [parts[0], in_hbm(parts[1]), in_hbm(parts[2])]
+
+    blocks = tokens // BLOCK
+    y_late, dx_late, grad_late = intra((blocks - 1,))
+    y_early, dx_early, grad_early = intra(tuple(range(blocks - 1)))
     (states,) = call(
         functools.partial(scan_kernel, sections, chunk),
-        [((sections, 2, chunk, width), f32)],
-        [VMEM, SMEM],
+        [((sections, 2 * chunk, width), f32)],
+        [VMEM],
         10**8,
-        4.0,
-    )(got, after)
+        4,
+    )(got)
     mine = lax.all_to_all(states, ("x", "zh"), 0, 0)
-    other = lax.ppermute(cross, "core", swap_cores)
-    came = lax.ppermute(mine, "core", swap_cores)
-    (piece,) = call(
-        carry_kernel,
-        [((tokens, width), f32)],
-        [SMEM, VMEM, VMEM, ANY, ANY],
+    keep, away = call(
+        functools.partial(carry_kernel, heads, chunk, tokens // (2 * spread)),
+        [((spread, tokens // (2 * spread), 2 * width), f32)] * 2,
+        [SMEM] + [VMEM] * 4 + [ANY] * 2,
         10**9,
-        16.0,
+        16,
         scratch_shapes=[
-            pltpu.VMEM((tokens, wide), f32),
-            pltpu.VMEM((tokens, wide), f32),
-            pltpu.SemaphoreType.DMA((tokens // BLOCK, 2)),
+            pltpu.VMEM(grad_late.shape, f32),
+            pltpu.VMEM(grad_early.shape, f32),
+            pltpu.SemaphoreType.DMA((2,)),
         ],
-    )(core, mine, came, in_hbm(own), other)
-    parts = lax.all_to_all(
-        piece.reshape(2 * spread, tokens // (2 * spread), width), ("y", "zl", "core"), 0, 0
-    )
+    )(core, mine, inputs, grad_out, rows, grad_late, grad_early)
+    other = lax.ppermute(away, "core", swap_cores)
+    parts = lax.all_to_all(keep + other, ("y", "zl"), 0, 0)
     outputs, grad_inputs = call(
-        functools.partial(finish_kernel, heads),
+        functools.partial(finish_kernel, heads, chunk),
         [((tokens, channels), bf16)] * 2,
-        [VMEM] * 6,
+        [VMEM] * 8,
         2 * 10**9,
-        12.0,
-    )(mine, write_proj, read_proj, rows, y_intra, dx_intra)
-    summed = jnp.sum(parts.reshape(spread, 2, -1, width), axis=0)
-    return (outputs, grad_inputs, summed[0], summed[1])
+        16,
+    )(mine, write_proj, read_proj, rows, y_late, y_early, dx_late, dx_early)
+    summed = jnp.sum(parts, axis=0)
+    return (outputs, grad_inputs, summed[:, :width], summed[:, width:])
 
 
 def solution(mesh, shape=(8, 4, 8, 2, 2)):

time: 97.2 us -> 91.3 us (0.939)
  starting transfers between devices: 35 us -> 15.8 us
  blocking collectives: 23.6 us -> 36.2 us
    all_to_all x2, starting transfers between devices: 31.2 us -> 13.9 us  [the longest x1 9.46 us: per_device(): parts = lax.all_to_all(keep + other, ('y', 'zl'), 0, 0)]
    all_to_all x1, blocking collectives: 23.6 us -> 36.2 us  [per_device(): lax.all_to_all(send.reshape(sections, stride, 1, width), ('x', 'zh'), 0, 0)]
    ppermute x2 -> x1, starting transfers between devices: 3.83 us -> 1.92 us  [per_device(): other = lax.ppermute(away, 'core', swap_cores)]
    pallas_call x4 -> x5, Pallas kernels: 14.8 us -> 15.6 us  [the longest x2 9.12 us: intra(): call(functools.partial(intra_kernel, heads, laters), [(size, f32) for siz...]
  transfers between devices with their start and end apart: 4 -> 3, of which waited for: 3 -> 3; matrix products, arithmetic and copies ran while one was open for 0% -> 0% of each run, Pallas kernels for 12% -> 14%
where the time goes in v4:
time: 91.3 us; the launch traced here: 90.9 us
  blocking collectives  36.2 us (40%)
  Pallas kernels  18.4 us (20%)
  waiting for transfers between devices  18.3 us (20%)
  starting transfers between devices  15.8 us (17%)
    all_to_all x1, blocking collectives, per_device(): lax.all_to_all(send.reshape(sections, stride, 1, width), ('x', 'zh'), 0, 0)  36.2 us
    all_to_all x1, waiting for transfers between devices, per_device(): parts = lax.all_to_all(keep + other, ('y', 'zl'), 0, 0)  11.7 us
    all_to_all x1, starting transfers between devices, per_device(): parts = lax.all_to_all(keep + other, ('y', 'zl'), 0, 0)  9.46 us
    pallas_call x2, Pallas kernels, intra(): call(functools.partial(intra_kernel, heads, laters), [(size, f32) for siz...  9.12 us
    all_to_all x1, waiting for transfers between devices, per_device(): mine = lax.all_to_all(states, ('x', 'zh'), 0, 0)  4.94 us
    all_to_all x1, starting transfers between devices, per_device(): mine = lax.all_to_all(states, ('x', 'zh'), 0, 0)  4.42 us
    pallas_call x1, Pallas kernels, per_device(): call(functools.partial(finish_kernel, heads, chunk), [((tokens, channels)...  3.29 us
    pallas_call x1, Pallas kernels, per_device(): call(functools.partial(local_kernel, sections), [((sections * stride, wid...  2.87 us
  transfers between devices with their start and end apart: 3, of which 3 were waited for; matrix products, arithmetic and copies ran while one was open for 0% of the time, Pallas kernels for 14%

profile of v4, /device:TPU:2, one launch (start us, length us, event | category | flops | bytes accessed | tf_op | source)
XLA Modules:
  0.0 90.9 jit_solution(15339012823060841257)
XLA Ops:
  0.6 2.9 %shard_map.84 = (f32[544,128]{1,0:T(8,128)S(1)}, f32[24,768]{1,0:T(8,128)S(1)}) custom-call(bf16[768,256]{1,0:T(8,128)(2,1)} %x_ref.5, bf16[768,256]{1,0:T(8,128)(2,1)} %g_ref.5, bf16[768,128]{1,0:T(8,128)(2,1)} %write_ref.5, bf16[768,128]{1,0:T(8,128)(2,1)} %read_ref.5, f32[4,768]{1,0:T(4,128)} %decay_hbm.1), custom_call_target="tpu_custom_call" | custom-call | flops 1000000000 | bytes 4194304 | tf_op jit(solution)/shard_map/pallas_call | solution.py:336
  3.5 0.0 copy-start.3
  3.5 36.2 %all_to_all.15 = f32[32,17,1,128]{3,2,1,0:T(1,128)S(1)} all-to-all(f32[32,17,1,128]{3,2,1,0:T(1,128)S(1)} %bitcast.4), channel_id=1, replica_groups=mesh['x'=8,'zh'=4,'y'=8,'zl'=2,'core'=2] {'x','zh'}, dimensions={0} | all-to-all | bytes 557056 | tf_op jit(solution)/shard_map/all_to_all | solution.py:351
  39.7 0.0 copy-start.1
  39.7 0.0 copy-start.2
  39.7 0.8 shard_map.85
  40.5 0.0 copy-start
  40.5 4.4 %all-to-all-start.1 = ((f32[32,16,128]{2,1,0:T(8,128)}), f32[32,16,128]{2,1,0:T(8,128)S(1)}, u32[]{:S(2)}, u32[]{:S(2)}) async-start(f32[32,16,128]{2,1,0:T(8,128)} %shard_map.85), calls=%async_computation.1 | async-start | bytes 524288 | tf_op jit(solution)/shard_map/all_to_all | solution.py:384
  44.9 0.0 copy-done.3
  44.9 0.0 copy-done.1
  44.9 0.0 copy-done.2
  44.9 0.0 copy-done
  44.9 4.7 %shard_map.86 = (f32[256,256]{1,0:T(8,128)S(1)}, f32[768,256]{1,0:T(8,128)}, f32[768,256]{1,0:T(8,128)}) custom-call(bf16[768,256]{1,0:T(8,128)(2,1)S(1)} %copy-done, bf16[768,256]{1,0:T(8,128)(2,1)S(1)} %copy-done.1, bf16[768,128]{1,0:T(8,128)(2,1)S(1)} %copy-done.2, bf16[768,128]{1,0:T(8,128)(2,1)S(1)} %copy-done.3, f32[24,768]{1,0:T(8,128)S(1)} %get-tuple-element.17.rows_ref), custom_call_target="tpu_custom_call" | custom-call | flops 4000000000 | bytes 4194304 | tf_op jit(solution)/shard_map/pallas_call | solution.py:360
  49.6 4.5 %shard_map.87 = (f32[512,256]{1,0:T(8,128)S(1)}, f32[512,256]{1,0:T(8,128)}, f32[512,256]{1,0:T(8,128)}) custom-call(bf16[768,256]{1,0:T(8,128)(2,1)S(1)} %copy-done, bf16[768,256]{1,0:T(8,128)(2,1)S(1)} %copy-done.1, bf16[768,128]{1,0:T(8,128)(2,1)S(1)} %copy-done.2, bf16[768,128]{1,0:T(8,128)(2,1)S(1)} %copy-done.3, f32[24,768]{1,0:T(8,128)S(1)} %get-tuple-element.17.rows_ref), custom_call_target="tpu_custom_call" | custom-call | flops 4000000000 | bytes 4194304 | tf_op jit(solution)/shard_map/pallas_call | solution.py:360
  54.1 4.9 %all-to-all-done.1.state_ref = f32[32,16,128]{2,1,0:T(8,128)S(1)} async-done(((f32[32,16,128]{2,1,0:T(8,128)}), f32[32,16,128]{2,1,0:T(8,128)S(1)}, u32[]{:S(2)}, u32[]{:S(2)}) %all-to-all-start.1) | async-done | bytes 262176 | tf_op jit(solution)/shard_map/all_to_all | solution.py:384
  59.0 2.4 %shard_map.89 = (f32[16,24,256]{2,1,0:T(8,128)S(1)}, f32[16,24,256]{2,1,0:T(8,128)S(1)}) custom-call(s32[1]{0:T(128)} %bitcast.2.core_ref, f32[32,16,128]{2,1,0:T(8,128)S(1)} %all-to-all-done.1.state_ref, bf16[768,256]{1,0:T(8,128)(2,1)S(1)} %copy-done, bf16[768,256]{1,0:T(8,128)(2,1)S(1)} %copy-done.1, f32[24,768]{1,0:T(8,128)S(1)} %get-tuple-element.17.rows_ref, ...), custom_call_target="tpu_custom_call" | custom-call | flops 1000000000 | bytes 4194304 | tf_op jit(solution)/shard_map/pallas_call | solution.py:385
  61.4 1.9 %collective-permute-start = (f32[16,24,256]{2,1,0:T(8,128)S(1)}, f32[16,24,256]{2,1,0:T(8,128)S(1)}, u32[]{:S(2)}, u32[]{:S(2)}) collective-permute-start(f32[16,24,256]{2,1,0:T(8,128)S(1)} %get-tuple-element.27), channel_id=1, source_target_pairs={{0,1},{1,0},{2,3},{3,2},{4,5},{5,4},{6,7},{7,6},{8,9},{9,8},{10,11... | collective-permute-start | bytes 1179656 | tf_op jit(solution)/shard_map/ppermute | solution.py:397
  63.3 1.7 %collective-permute-done = f32[16,24,256]{2,1,0:T(8,128)S(1)} collective-permute-done((f32[16,24,256]{2,1,0:T(8,128)S(1)}, f32[16,24,256]{2,1,0:T(8,128)S(1)}, u32[]{:S(2)}, u32[]{:S(2)}) %collective-permute-start) | collective-permute-done | bytes 393248 | tf_op jit(solution)/shard_map/ppermute | solution.py:397
  65.0 0.8 add.3
  65.8 9.5 %all-to-all-start.2 = ((f32[16,24,256]{2,1,0:T(8,128)}), f32[16,24,256]{2,1,0:T(8,128)S(1)}, u32[]{:S(2)}, u32[]{:S(2)}) async-start(f32[16,24,256]{2,1,0:T(8,128)} %add.3), calls=%async_computation.2 | async-start | bytes 786432 | tf_op jit(solution)/shard_map/all_to_all | solution.py:398
  75.3 3.3 %shard_map.88 = (bf16[768,256]{1,0:T(8,128)(2,1)}, bf16[768,256]{1,0:T(8,128)(2,1)}) custom-call(f32[32,16,128]{2,1,0:T(8,128)S(1)} %all-to-all-done.1.state_ref, bf16[768,128]{1,0:T(8,128)(2,1)S(1)} %copy-done.2, bf16[768,128]{1,0:T(8,128)(2,1)S(1)} %copy-done.3, f32[24,768]{1,0:T(8,128)S(1)} %get-tuple-element.17.rows_ref, ...), custom_call_target="tpu_custom_call" | custom-call | flops 2000000000 | bytes 4194304 | tf_op jit(solution)/shard_map/pallas_call | solution.py:399
  78.6 11.7 %all-to-all-done.2 = f32[16,24,256]{2,1,0:T(8,128)S(1)} async-done(((f32[16,24,256]{2,1,0:T(8,128)}), f32[16,24,256]{2,1,0:T(8,128)S(1)}, u32[]{:S(2)}, u32[]{:S(2)}) %all-to-all-start.2) | async-done | bytes 393248 | tf_op jit(solution)/shard_map/all_to_all | solution.py:398
  90.3 0.6 fusion
  (1 shorter events, 0.0 us)
Async XLA Ops:
  3.5 41.4 %copy-start.3 = (bf16[768,128]{1,0:T(8,128)(2,1)S(1)}, bf16[768,128]{1,0:T(8,128)(2,1)}, u32[]{:S(2)}) copy-start(bf16[768,128]{1,0:T(8,128)(2,1)} %read_ref.5) | copy-start | bytes 589828
  39.7 5.2 %copy-start.1 = (bf16[768,256]{1,0:T(8,128)(2,1)S(1)}, bf16[768,256]{1,0:T(8,128)(2,1)}, u32[]{:S(2)}) copy-start(bf16[768,256]{1,0:T(8,128)(2,1)} %g_ref.5) | copy-start | bytes 1179652
  39.7 5.2 %copy-start.2 = (bf16[768,128]{1,0:T(8,128)(2,1)S(1)}, bf16[768,128]{1,0:T(8,128)(2,1)}, u32[]{:S(2)}) copy-start(bf16[768,128]{1,0:T(8,128)(2,1)} %write_ref.5) | copy-start | bytes 589828
  40.5 4.5 %copy-start = (bf16[768,256]{1,0:T(8,128)(2,1)S(1)}, bf16[768,256]{1,0:T(8,128)(2,1)}, u32[]{:S(2)}) copy-start(bf16[768,256]{1,0:T(8,128)(2,1)} %x_ref.5) | copy-start | bytes 1179652
  40.5 18.5 %all-to-all-start.1 = ((f32[32,16,128]{2,1,0:T(8,128)}), f32[32,16,128]{2,1,0:T(8,128)S(1)}, u32[]{:S(2)}, u32[]{:S(2)}) async-start(f32[32,16,128]{2,1,0:T(8,128)} %shard_map.85), calls=%async_computation.1 | async-start | bytes 524288 | tf_op jit(solution)/shard_map/all_to_all | solution.py:384
  61.4 3.6 %collective-permute-start = (f32[16,24,256]{2,1,0:T(8,128)S(1)}, f32[16,24,256]{2,1,0:T(8,128)S(1)}, u32[]{:S(2)}, u32[]{:S(2)}) collective-permute-start(f32[16,24,256]{2,1,0:T(8,128)S(1)} %get-tuple-element.27), channel_id=1, source_target_pairs={{0,1},{1,0},{2,3},{3,2},{4,5},{5,4},{6,7},{7,6},{8,9},{9,8},{10,11... | collective-permute-start | bytes 1179656 | tf_op jit(solution)/shard_map/ppermute | solution.py:397
  65.8 24.4 %all-to-all-start.2 = ((f32[16,24,256]{2,1,0:T(8,128)}), f32[16,24,256]{2,1,0:T(8,128)S(1)}, u32[]{:S(2)}, u32[]{:S(2)}) async-start(f32[16,24,256]{2,1,0:T(8,128)} %add.3), calls=%async_computation.2 | async-start | bytes 786432 | tf_op jit(solution)/shard_map/all_to_all | solution.py:398

commit v5 on v4

--- a/solution.py
+++ b/solution.py
@@ -13,6 +13,7 @@
 SMEM = pl.BlockSpec(memory_space=pltpu.SMEM)
 ANY = pl.BlockSpec(memory_space=pl.ANY)
 BLOCK = 256
+GRANT = (52, 50)
 
 
 def dot(a, b, dims):
@@ -145,14 +146,15 @@
     write_ref,
     read_ref,
     rows_ref,
-    y_hbm,
-    dx_hbm,
-    grad_hbm,
-    y_ref,
-    dx_ref,
-    grad_ref,
-    left,
+    *rest,
 ):
+    joins = len(rest) == 9
+    if joins:
+        before_hbm, y_hbm, dx_hbm, grad_ref, y_ref, dx_ref, before_ref, left, arrived = rest
+        before = pltpu.make_async_copy(before_hbm, before_ref, arrived)
+        before.start()
+    else:
+        y_hbm, dx_hbm, grad_hbm, y_ref, dx_ref, grad_ref, left = rest
     channels = x_ref.shape[1]
     head_size = channels // heads
     width = write_ref.shape[1]
@@ -199,10 +201,14 @@
             grad_ref[t, width:] += dot(high, write, ((1,), (0,))) + dot(low, write, ((1,), (0,)))
             if place == len(laters) - 1:
                 leave(dx_ref, dx_hbm, earlier * BLOCK, BLOCK)
-                if earlier < later:
+                if earlier < later and not joins:
                     leave(grad_ref, grad_hbm, earlier * BLOCK, BLOCK)
         leave(y_ref, y_hbm, place * BLOCK, BLOCK)
-    leave(grad_ref, grad_hbm, laters[-1] * BLOCK, BLOCK)
+    if joins:
+        before.wait()
+        grad_ref[...] += before_ref[...]
+    else:
+        leave(grad_ref, grad_hbm, laters[-1] * BLOCK, BLOCK)
     for copy in started:
         copy.wait()
 
@@ -235,32 +241,17 @@
     x_ref,
     g_ref,
     rows_ref,
-    late_hbm,
-    early_hbm,
+    intra_ref,
     keep_ref,
     send_ref,
-    late_ref,
-    early_ref,
-    arrived,
 ):
-    copies = [
-        pltpu.make_async_copy(late_hbm, late_ref, arrived.at[0]),
-        pltpu.make_async_copy(early_hbm, early_ref, arrived.at[1]),
-    ]
-    for copy in copies:
-        copy.start()
     forward, backward = states_of(state_ref, chunk)
     width = forward.shape[1]
     count = keep_ref.shape[0]
     cols = rows_ref[...].T
     of_write = carried(x_ref[...], backward, cols[:, 16:24], heads)
     of_read = carried(g_ref[...], forward, cols[:, 8:16], heads)
-    for copy in copies:
-        copy.wait()
-    known = early_ref.shape[0]
-    late = late_ref[...]
-    intra = jnp.concatenate([late[:known] + early_ref[...], late[known:]], axis=0)
-    whole = jnp.concatenate([of_write, of_read], axis=1) + intra
+    whole = jnp.concatenate([of_write, of_read], axis=1) + intra_ref[...]
     whole = whole.reshape(count, 2, group, 2 * width)
 
     @pl.when(core_ref[0] == 0)
@@ -272,6 +263,19 @@
     def _():
         keep_ref[...] = whole[:, 1]
         send_ref[...] = whole[:, 0]
+
+
+def join_kernel(keep_ref, other_ref, out_hbm, out_ref, left):
+    pieces = left.shape[0]
+    count = keep_ref.shape[0] // pieces
+    copies = []
+    for piece in range(pieces):
+        at = pl.ds(piece * count, count)
+        out_ref[at] = keep_ref[at] + other_ref[at]
+        copies.append(pltpu.make_async_copy(out_ref.at[at], out_hbm.at[at], left.at[piece]))
+        copies[-1].start()
+    for copy in copies:
+        copy.wait()
 
 
 def finish_kernel(
@@ -333,47 +337,53 @@
     stride = 2 * chunk + 1
     core = lax.axis_index("core").reshape(1)
     swap_cores = [(0, 1), (1, 0)]
-    send, rows = call(
+    send, rows, inputs_near, grad_near, write_near, read_near = call(
         functools.partial(local_kernel, sections),
-        [((sections * stride, width), f32), ((24, tokens), f32)],
+        [
+            ((sections * stride, width), f32),
+            ((24, tokens), f32),
+            (inputs.shape, bf16),
+            (inputs.shape, bf16),
+            (write_proj.shape, bf16),
+            (write_proj.shape, bf16),
+        ],
         [ANY] * 5,
         10**9,
         16,
         scratch_shapes=[
-            pltpu.VMEM(inputs.shape, bf16),
-            pltpu.VMEM(inputs.shape, bf16),
-            pltpu.VMEM(write_proj.shape, bf16),
-            pltpu.VMEM(write_proj.shape, bf16),
             pltpu.VMEM(log_decay.shape, f32),
             pltpu.SemaphoreType.DMA((5,)),
         ],
     )(*(in_hbm(value) for value in (inputs, grad_out, write_proj, read_proj, log_decay)))
+    inputs, grad_out, write_proj, read_proj = inputs_near, grad_near, write_near, read_near
     got = lax.all_to_all(send.reshape(sections, stride, 1, width), ("x", "zh"), 0, 0)
     got = got.reshape(sections * stride, width)
 
-    def intra(laters):
+    def intra(laters, before=None):
+        joins = before is not None
+        reach = (laters[-1] + 1) * BLOCK
         sizes = (
             (len(laters) * BLOCK, channels),
-            ((laters[-1] + 1) * BLOCK, channels),
-            ((laters[-1] + 1) * BLOCK, 2 * width),
+            (reach, channels),
+            (tokens if joins else reach, 2 * width),
         )
+        scratch = [pltpu.VMEM(size, f32) for size in sizes]
+        copies = pltpu.SemaphoreType.DMA((len(laters) + 2 * (laters[-1] + 1),))
+        scratch += [copies, pltpu.SemaphoreType.DMA(())] if joins else [copies]
         parts = call(
             functools.partial(intra_kernel, heads, laters),
             [(size, f32) for size in sizes],
-            [VMEM] * 5,
+            [VMEM] * 5 + [ANY] * joins,
             4 * 10**9,
-            52,
-            out_specs=[ANY] * 3,
-            scratch_shapes=[
-                *(pltpu.VMEM(size, f32) for size in sizes),
-                pltpu.SemaphoreType.DMA((len(laters) + 2 * (laters[-1] + 1),)),
-            ],
-        )(inputs, grad_out, write_proj, read_proj, rows)
-        return [parts[0], in_hbm(parts[1]), in_hbm(parts[2])]
+            GRANT[joins],
+            out_specs=[ANY, ANY, VMEM if joins else ANY],
+            scratch_shapes=scratch,
+        )(inputs, grad_out, write_proj, read_proj, rows, *([in_hbm(before)] if joins else []))
+        return [parts[0], in_hbm(parts[1]), parts[2]]
 
     blocks = tokens // BLOCK
     y_late, dx_late, grad_late = intra((blocks - 1,))
-    y_early, dx_early, grad_early = intra(tuple(range(blocks - 1)))
+    y_early, dx_early, grad_intra = intra(tuple(range(blocks - 1)), grad_late)
     (states,) = call(
         functools.partial(scan_kernel, sections, chunk),
         [((sections, 2 * chunk, width), f32)],
@@ -385,17 +395,21 @@
     keep, away = call(
         functools.partial(carry_kernel, heads, chunk, tokens // (2 * spread)),
         [((spread, tokens // (2 * spread), 2 * width), f32)] * 2,
-        [SMEM] + [VMEM] * 4 + [ANY] * 2,
+        [SMEM] + [VMEM] * 5,
         10**9,
         16,
-        scratch_shapes=[
-            pltpu.VMEM(grad_late.shape, f32),
-            pltpu.VMEM(grad_early.shape, f32),
-            pltpu.SemaphoreType.DMA((2,)),
-        ],
-    )(core, mine, inputs, grad_out, rows, grad_late, grad_early)
+    )(core, mine, inputs, grad_out, rows, grad_intra)
     other = lax.ppermute(away, "core", swap_cores)
-    parts = lax.all_to_all(keep + other, ("y", "zl"), 0, 0)
+    (joined,) = call(
+        join_kernel,
+        [(keep.shape, f32)],
+        [VMEM] * 2,
+        10**7,
+        8,
+        out_specs=[ANY],
+        scratch_shapes=[pltpu.VMEM(keep.shape, f32), pltpu.SemaphoreType.DMA((2,))],
+    )(keep, other)
+    parts = lax.all_to_all(joined, ("y", "zl"), 0, 0)
     outputs, grad_inputs = call(
         functools.partial(finish_kernel, heads, chunk),
         [((tokens, channels), bf16)] * 2,

time: 91.3 us -> 89.8 us (0.984)
  Pallas kernels: 18.4 us -> 17.3 us
    pallas_call x1, Pallas kernels: 2.37 us -> 1.12 us  [per_device(): call(functools.partial(carry_kernel, heads, chunk, tokens // (2 * spread)...]
  transfers between devices with their start and end apart: 3 -> 3, of which waited for: 3 -> 3; matrix products, arithmetic and copies ran while one was open for 0% -> 0% of each run, Pallas kernels for 14% -> 13%
where the time goes in v5:
time: 89.8 us; the launch traced here: 89.4 us
  blocking collectives  36 us (40%)
  waiting for transfers between devices  18.2 us (20%)
  Pallas kernels  17.3 us (19%)
  starting transfers between devices  15.7 us (17%)
  local copies, waits for them, and re-layouts  1.4 us (2%)
    all_to_all x1, blocking collectives, per_device(): lax.all_to_all(send.reshape(sections, stride, 1, width), ('x', 'zh'), 0, 0)  36 us
    all_to_all x1, waiting for transfers between devices, per_device(): parts = lax.all_to_all(joined, ('y', 'zl'), 0, 0)  11.7 us
    all_to_all x1, starting transfers between devices, per_device(): parts = lax.all_to_all(joined, ('y', 'zl'), 0, 0)  9.47 us
    pallas_call x2, Pallas kernels, intra(): call(functools.partial(intra_kernel, heads, laters), [(size, f32) for siz...  8.45 us
    all_to_all x1, waiting for transfers between devices, per_device(): mine = lax.all_to_all(states, ('x', 'zh'), 0, 0)  4.85 us
    all_to_all x1, starting transfers between devices, per_device(): mine = lax.all_to_all(states, ('x', 'zh'), 0, 0)  4.29 us
    pallas_call x1, Pallas kernels, per_device(): call(functools.partial(finish_kernel, heads, chunk), [((tokens, channels)...  3.25 us
    pallas_call x1, Pallas kernels, per_device(): call(functools.partial(local_kernel, sections), [((sections * stride, wid...  2.87 us
  transfers between devices with their start and end apart: 3, of which 3 were waited for; matrix products, arithmetic and copies ran while one was open for 0% of the time, Pallas kernels for 13%

profile of v5, /device:TPU:2, one launch (start us, length us, event | category | flops | bytes accessed | tf_op | source)
XLA Modules:
  0.0 89.4 jit_solution(9976782127376197015)
XLA Ops:
  0.6 2.9 %shard_map.84 = (f32[544,128]{1,0:T(8,128)S(1)}, f32[24,768]{1,0:T(8,128)S(1)}, bf16[768,256]{1,0:T(8,128)(2,1)S(1)}, bf16[768,256]{1,0:T(8,128)(2,1)S(1)}, bf16...) custom-call(bf16[768,256]{1,0:T(8,128)(2,1)} %x_hbm.1, bf16[768,256]{1,0:T(8,128)(2,1)} %g_hbm.1, ...), custom_call_target="tpu_custom_call" | custom-call | flops 1000000000 | bytes 4194304 | tf_op jit(solution)/shard_map/pallas_call | solution.py:340
  3.5 36.0 %all_to_all.15 = f32[32,17,1,128]{3,2,1,0:T(1,128)S(1)} all-to-all(f32[32,17,1,128]{3,2,1,0:T(1,128)S(1)} %bitcast.4), channel_id=1, replica_groups=mesh['x'=8,'zh'=4,'y'=8,'zl'=2,'core'=2] {'x','zh'}, dimensions={0} | all-to-all | bytes 557056 | tf_op jit(solution)/shard_map/all_to_all | solution.py:359
  39.5 0.8 shard_map.85
  40.3 4.3 %all-to-all-start.1 = ((f32[32,16,128]{2,1,0:T(8,128)}), f32[32,16,128]{2,1,0:T(8,128)S(1)}, u32[]{:S(2)}, u32[]{:S(2)}) async-start(f32[32,16,128]{2,1,0:T(8,128)} %shard_map.85), calls=%async_computation.1 | async-start | bytes 524288 | tf_op jit(solution)/shard_map/all_to_all | solution.py:394
  44.6 4.6 %shard_map.86 = (f32[256,256]{1,0:T(8,128)S(1)}, f32[768,256]{1,0:T(8,128)}, f32[768,256]{1,0:T(8,128)}) custom-call(bf16[768,256]{1,0:T(8,128)(2,1)S(1)} %get-tuple-element.24.x_ref, bf16[768,256]{1,0:T(8,128)(2,1)S(1)} %get-tuple-element.25.g_ref, bf16[768,128]{1,0:T(8,128)(2,1)S(1)} %get-tuple-element.21.write_ref, ...), custom_call_target="tpu_custom_call" | custom-call | flops 4000000000 | bytes 4194304 | tf_op jit(solution)/shard_map/pallas_call | solution.py:373
  49.3 3.8 %shard_map.87 = (f32[512,256]{1,0:T(8,128)S(1)}, f32[512,256]{1,0:T(8,128)S(1)}, f32[768,256]{1,0:T(8,128)S(1)}) custom-call(bf16[768,256]{1,0:T(8,128)(2,1)S(1)} %get-tuple-element.24.x_ref, bf16[768,256]{1,0:T(8,128)(2,1)S(1)} %get-tuple-element.25.g_ref, bf16[768,128]{1,0:T(8,128)(2,1)S(1)} %get-tuple-element.21.write_ref, ...), custom_call_target="tpu_custom_call" | custom-call | flops 4000000000 | bytes 4194304 | tf_op jit(solution)/shard_map/pallas_call | solution.py:373
  53.1 0.0 copy-start
  53.1 0.8 copy-done
  53.9 4.8 %all-to-all-done.1.state_ref = f32[32,16,128]{2,1,0:T(8,128)S(1)} async-done(((f32[32,16,128]{2,1,0:T(8,128)}), f32[32,16,128]{2,1,0:T(8,128)S(1)}, u32[]{:S(2)}, u32[]{:S(2)}) %all-to-all-start.1) | async-done | bytes 262176 | tf_op jit(solution)/shard_map/all_to_all | solution.py:394
  58.7 1.1 %shard_map.89 = (f32[16,24,256]{2,1,0:T(8,128)S(1)}, f32[16,24,256]{2,1,0:T(8,128)S(1)}) custom-call(s32[1]{0:T(128)} %bitcast.2.core_ref, f32[32,16,128]{2,1,0:T(8,128)S(1)} %all-to-all-done.1.state_ref, bf16[768,256]{1,0:T(8,128)(2,1)S(1)} %get-tuple-element.24.x_ref, bf16[768,256]{1,0:T(8,128)(2,1)S(1)} %get-tuple-element.25.g_ref, ...), custom_call_target="tpu_custom_call" | custom-call | flops 1000000000 | bytes 4194304 | tf_op jit(solution)/shard_map/pallas_call | solution.py:395
  59.9 1.9 %collective-permute-start = (f32[16,24,256]{2,1,0:T(8,128)S(1)}, f32[16,24,256]{2,1,0:T(8,128)S(1)}, u32[]{:S(2)}, u32[]{:S(2)}) collective-permute-start(f32[16,24,256]{2,1,0:T(8,128)S(1)} %get-tuple-element.35), channel_id=1, source_target_pairs={{0,1},{1,0},{2,3},{3,2},{4,5},{5,4},{6,7},{7,6},{8,9},{9,8},{10,11... | collective-permute-start | bytes 1179656 | tf_op jit(solution)/shard_map/ppermute | solution.py:402
  61.8 1.7 %collective-permute-done.other_ref = f32[16,24,256]{2,1,0:T(8,128)S(1)} collective-permute-done((f32[16,24,256]{2,1,0:T(8,128)S(1)}, f32[16,24,256]{2,1,0:T(8,128)S(1)}, u32[]{:S(2)}, u32[]{:S(2)}) %collective-permute-start) | collective-permute-done | bytes 393248 | tf_op jit(solution)/shard_map/ppermute | solution.py:402
  63.5 0.8 shard_map.90
  64.3 9.5 %all-to-all-start.2 = ((f32[16,24,256]{2,1,0:T(8,128)}), f32[16,24,256]{2,1,0:T(8,128)S(1)}, u32[]{:S(2)}, u32[]{:S(2)}) async-start(f32[16,24,256]{2,1,0:T(8,128)} %shard_map.90), calls=%async_computation.2 | async-start | bytes 786432 | tf_op jit(solution)/shard_map/all_to_all | solution.py:412
  73.8 3.3 %shard_map.88 = (bf16[768,256]{1,0:T(8,128)(2,1)}, bf16[768,256]{1,0:T(8,128)(2,1)}) custom-call(f32[32,16,128]{2,1,0:T(8,128)S(1)} %all-to-all-done.1.state_ref, bf16[768,128]{1,0:T(8,128)(2,1)S(1)} %get-tuple-element.21.write_ref, bf16[768,128]{1,0:T(8,128)(2,1)S(1)} %get-tuple-element.22.read_ref, f32[24,768]{1,0:T(8,128)S(1)} %get-tuple-element.23.rows_ref, ...), custom_call_target="tpu_custom_call" | custom-call | flops 2000000000 | bytes 4194304 | tf_op jit(solution)/shard_map/pallas_call | solution.py:413
  77.0 11.7 %all-to-all-done.2 = f32[16,24,256]{2,1,0:T(8,128)S(1)} async-done(((f32[16,24,256]{2,1,0:T(8,128)}), f32[16,24,256]{2,1,0:T(8,128)S(1)}, u32[]{:S(2)}, u32[]{:S(2)}) %all-to-all-start.2) | async-done | bytes 393248 | tf_op jit(solution)/shard_map/all_to_all | solution.py:412
  88.8 0.6 fusion
  (1 shorter events, 0.0 us)
Async XLA Ops:
  40.3 18.4 %all-to-all-start.1 = ((f32[32,16,128]{2,1,0:T(8,128)}), f32[32,16,128]{2,1,0:T(8,128)S(1)}, u32[]{:S(2)}, u32[]{:S(2)}) async-start(f32[32,16,128]{2,1,0:T(8,128)} %shard_map.85), calls=%async_computation.1 | async-start | bytes 524288 | tf_op jit(solution)/shard_map/all_to_all | solution.py:394
  53.1 0.8 copy-start
  59.9 3.6 %collective-permute-start = (f32[16,24,256]{2,1,0:T(8,128)S(1)}, f32[16,24,256]{2,1,0:T(8,128)S(1)}, u32[]{:S(2)}, u32[]{:S(2)}) collective-permute-start(f32[16,24,256]{2,1,0:T(8,128)S(1)} %get-tuple-element.35), channel_id=1, source_target_pairs={{0,1},{1,0},{2,3},{3,2},{4,5},{5,4},{6,7},{7,6},{8,9},{9,8},{10,11... | collective-permute-start | bytes 1179656 | tf_op jit(solution)/shard_map/ppermute | solution.py:402
  64.3 24.4 %all-to-all-start.2 = ((f32[16,24,256]{2,1,0:T(8,128)}), f32[16,24,256]{2,1,0:T(8,128)S(1)}, u32[]{:S(2)}, u32[]{:S(2)}) async-start(f32[16,24,256]{2,1,0:T(8,128)} %shard_map.90), calls=%async_computation.2 | async-start | bytes 786432 | tf_op jit(solution)/shard_map/all_to_all | solution.py:412

commit v6 on v5

--- a/solution.py
+++ b/solution.py
@@ -41,7 +41,7 @@
     write_hbm,
     read_hbm,
     decay_hbm,
-    send_ref,
+    send_hbm,
     rows_ref,
     x_ref,
     g_ref,
@@ -49,6 +49,8 @@
     read_ref,
     decay_ref,
     arrived,
+    send_ref,
+    left,
 ):
     pairs = (
         (decay_hbm, decay_ref),
@@ -117,6 +119,14 @@
                 if flow == 0:
                     at = base + 2 * chunk
                     send_ref[at : at + 1, :] = jnp.broadcast_to(total[head : head + 1], (1, width))
+            if flow == 1:
+                count = per_head * (2 * chunk + 1)
+                at = pl.ds(head * count, count)
+                leaving = pltpu.make_async_copy(send_ref.at[at], send_hbm.at[at], left.at[head])
+                leaving.start()
+                copies.append(leaving)
+    for copy in copies[len(pairs) :]:
+        copy.wait()
 
 
 def scan_kernel(sections, chunk, got_ref, out_ref):
@@ -353,7 +363,10 @@
         scratch_shapes=[
             pltpu.VMEM(log_decay.shape, f32),
             pltpu.SemaphoreType.DMA((5,)),
+            pltpu.VMEM((sections * stride, width), f32),
+            pltpu.SemaphoreType.DMA((heads,)),
         ],
+        out_specs=[ANY] + [VMEM] * 5,
     )(*(in_hbm(value) for value in (inputs, grad_out, write_proj, read_proj, log_decay)))
     inputs, grad_out, write_proj, read_proj = inputs_near, grad_near, write_near, read_near
     got = lax.all_to_all(send.reshape(sections, stride, 1, width), ("x", "zh"), 0, 0)

time: 89.8 us -> 90.7 us (1.010)
    pallas_call x1, Pallas kernels: 2.87 us -> 3.8 us  [per_device(): call(functools.partial(local_kernel, sections), [((sections * stride, wid...]
where the time goes in v6:
time: 90.7 us; the launch traced here: 90.3 us
  blocking collectives  36 us (40%)
  Pallas kernels  18.2 us (20%)
  waiting for transfers between devices  18.2 us (20%)
  starting transfers between devices  15.7 us (17%)
  local copies, waits for them, and re-layouts  1.4 us (2%)
    all_to_all x1, blocking collectives, per_device(): lax.all_to_all(send.reshape(sections, stride, 1, width), ('x', 'zh'), 0, 0)  36 us
    all_to_all x1, waiting for transfers between devices, per_device(): parts = lax.all_to_all(joined, ('y', 'zl'), 0, 0)  11.7 us
    all_to_all x1, starting transfers between devices, per_device(): parts = lax.all_to_all(joined, ('y', 'zl'), 0, 0)  9.47 us
    pallas_call x2, Pallas kernels, intra(): call(functools.partial(intra_kernel, heads, laters), [(size, f32) for siz...  8.46 us
    all_to_all x1, waiting for transfers between devices, per_device(): mine = lax.all_to_all(states, ('x', 'zh'), 0, 0)  4.83 us
    all_to_all x1, starting transfers between devices, per_device(): mine = lax.all_to_all(states, ('x', 'zh'), 0, 0)  4.29 us
    pallas_call x1, Pallas kernels, per_device(): call(functools.partial(local_kernel, sections), [((sections * stride, wid...  3.8 us
    pallas_call x1, Pallas kernels, per_device(): call(functools.partial(finish_kernel, heads, chunk), [((tokens, channels)...  3.26 us
  transfers between devices with their start and end apart: 3, of which 3 were waited for; matrix products, arithmetic and copies ran while one was open for 0% of the time, Pallas kernels for 13%

profile of v6, /device:TPU:2, one launch (start us, length us, event | category | flops | bytes accessed | tf_op | source)
XLA Modules:
  0.0 90.3 jit_solution(17659793028280683403)
XLA Ops:
  0.6 3.8 %shard_map.84 = (f32[544,128]{1,0:T(8,128)S(1)}, f32[24,768]{1,0:T(8,128)S(1)}, bf16[768,256]{1,0:T(8,128)(2,1)S(1)}, bf16[768,256]{1,0:T(8,128)(2,1)S(1)}, bf16...) custom-call(bf16[768,256]{1,0:T(8,128)(2,1)} %x_hbm.1, bf16[768,256]{1,0:T(8,128)(2,1)} %g_hbm.1, ...), custom_call_target="tpu_custom_call" | custom-call | flops 1000000000 | bytes 4194304 | tf_op jit(solution)/shard_map/pallas_call | solution.py:350
  4.4 36.0 %all_to_all.15 = f32[32,17,1,128]{3,2,1,0:T(1,128)S(1)} all-to-all(f32[32,17,1,128]{3,2,1,0:T(1,128)S(1)} %bitcast.4), channel_id=1, replica_groups=mesh['x'=8,'zh'=4,'y'=8,'zl'=2,'core'=2] {'x','zh'}, dimensions={0} | all-to-all | bytes 557056 | tf_op jit(solution)/shard_map/all_to_all | solution.py:372
  40.5 0.8 shard_map.85
  41.2 4.3 %all-to-all-start.1 = ((f32[32,16,128]{2,1,0:T(8,128)}), f32[32,16,128]{2,1,0:T(8,128)S(1)}, u32[]{:S(2)}, u32[]{:S(2)}) async-start(f32[32,16,128]{2,1,0:T(8,128)} %shard_map.85), calls=%async_computation.1 | async-start | bytes 524288 | tf_op jit(solution)/shard_map/all_to_all | solution.py:407
  45.5 4.7 %shard_map.86 = (f32[256,256]{1,0:T(8,128)S(1)}, f32[768,256]{1,0:T(8,128)}, f32[768,256]{1,0:T(8,128)}) custom-call(bf16[768,256]{1,0:T(8,128)(2,1)S(1)} %get-tuple-element.24.x_ref, bf16[768,256]{1,0:T(8,128)(2,1)S(1)} %get-tuple-element.25.g_ref, bf16[768,128]{1,0:T(8,128)(2,1)S(1)} %get-tuple-element.21.write_ref, ...), custom_call_target="tpu_custom_call" | custom-call | flops 4000000000 | bytes 4194304 | tf_op jit(solution)/shard_map/pallas_call | solution.py:386
  50.2 3.8 %shard_map.87 = (f32[512,256]{1,0:T(8,128)S(1)}, f32[512,256]{1,0:T(8,128)S(1)}, f32[768,256]{1,0:T(8,128)S(1)}) custom-call(bf16[768,256]{1,0:T(8,128)(2,1)S(1)} %get-tuple-element.24.x_ref, bf16[768,256]{1,0:T(8,128)(2,1)S(1)} %get-tuple-element.25.g_ref, bf16[768,128]{1,0:T(8,128)(2,1)S(1)} %get-tuple-element.21.write_ref, ...), custom_call_target="tpu_custom_call" | custom-call | flops 4000000000 | bytes 4194304 | tf_op jit(solution)/shard_map/pallas_call | solution.py:386
  54.0 0.0 copy-start
  54.0 0.8 copy-done
  54.8 4.8 %all-to-all-done.1.state_ref = f32[32,16,128]{2,1,0:T(8,128)S(1)} async-done(((f32[32,16,128]{2,1,0:T(8,128)}), f32[32,16,128]{2,1,0:T(8,128)S(1)}, u32[]{:S(2)}, u32[]{:S(2)}) %all-to-all-start.1) | async-done | bytes 262176 | tf_op jit(solution)/shard_map/all_to_all | solution.py:407
  59.7 1.1 %shard_map.89 = (f32[16,24,256]{2,1,0:T(8,128)S(1)}, f32[16,24,256]{2,1,0:T(8,128)S(1)}) custom-call(s32[1]{0:T(128)} %bitcast.2.core_ref, f32[32,16,128]{2,1,0:T(8,128)S(1)} %all-to-all-done.1.state_ref, bf16[768,256]{1,0:T(8,128)(2,1)S(1)} %get-tuple-element.24.x_ref, bf16[768,256]{1,0:T(8,128)(2,1)S(1)} %get-tuple-element.25.g_ref, ...), custom_call_target="tpu_custom_call" | custom-call | flops 1000000000 | bytes 4194304 | tf_op jit(solution)/shard_map/pallas_call | solution.py:408
  60.8 1.9 %collective-permute-start = (f32[16,24,256]{2,1,0:T(8,128)S(1)}, f32[16,24,256]{2,1,0:T(8,128)S(1)}, u32[]{:S(2)}, u32[]{:S(2)}) collective-permute-start(f32[16,24,256]{2,1,0:T(8,128)S(1)} %get-tuple-element.35), channel_id=1, source_target_pairs={{0,1},{1,0},{2,3},{3,2},{4,5},{5,4},{6,7},{7,6},{8,9},{9,8},{10,11... | collective-permute-start | bytes 1179656 | tf_op jit(solution)/shard_map/ppermute | solution.py:415
  62.7 1.7 %collective-permute-done.other_ref = f32[16,24,256]{2,1,0:T(8,128)S(1)} collective-permute-done((f32[16,24,256]{2,1,0:T(8,128)S(1)}, f32[16,24,256]{2,1,0:T(8,128)S(1)}, u32[]{:S(2)}, u32[]{:S(2)}) %collective-permute-start) | collective-permute-done | bytes 393248 | tf_op jit(solution)/shard_map/ppermute | solution.py:415
  64.4 0.8 shard_map.90
  65.2 9.5 %all-to-all-start.2 = ((f32[16,24,256]{2,1,0:T(8,128)}), f32[16,24,256]{2,1,0:T(8,128)S(1)}, u32[]{:S(2)}, u32[]{:S(2)}) async-start(f32[16,24,256]{2,1,0:T(8,128)} %shard_map.90), calls=%async_computation.2 | async-start | bytes 786432 | tf_op jit(solution)/shard_map/all_to_all | solution.py:425
  74.7 3.3 %shard_map.88 = (bf16[768,256]{1,0:T(8,128)(2,1)}, bf16[768,256]{1,0:T(8,128)(2,1)}) custom-call(f32[32,16,128]{2,1,0:T(8,128)S(1)} %all-to-all-done.1.state_ref, bf16[768,128]{1,0:T(8,128)(2,1)S(1)} %get-tuple-element.21.write_ref, bf16[768,128]{1,0:T(8,128)(2,1)S(1)} %get-tuple-element.22.read_ref, f32[24,768]{1,0:T(8,128)S(1)} %get-tuple-element.23.rows_ref, ...), custom_call_target="tpu_custom_call" | custom-call | flops 2000000000 | bytes 4194304 | tf_op jit(solution)/shard_map/pallas_call | solution.py:426
  77.9 11.7 %all-to-all-done.2 = f32[16,24,256]{2,1,0:T(8,128)S(1)} async-done(((f32[16,24,256]{2,1,0:T(8,128)}), f32[16,24,256]{2,1,0:T(8,128)S(1)}, u32[]{:S(2)}, u32[]{:S(2)}) %all-to-all-start.2) | async-done | bytes 393248 | tf_op jit(solution)/shard_map/all_to_all | solution.py:425
  89.7 0.6 fusion
  (1 shorter events, 0.0 us)
Async XLA Ops:
  41.2 18.4 %all-to-all-start.1 = ((f32[32,16,128]{2,1,0:T(8,128)}), f32[32,16,128]{2,1,0:T(8,128)S(1)}, u32[]{:S(2)}, u32[]{:S(2)}) async-start(f32[32,16,128]{2,1,0:T(8,128)} %shard_map.85), calls=%async_computation.1 | async-start | bytes 524288 | tf_op jit(solution)/shard_map/all_to_all | solution.py:407
  54.0 0.8 copy-start
  60.8 3.6 %collective-permute-start = (f32[16,24,256]{2,1,0:T(8,128)S(1)}, f32[16,24,256]{2,1,0:T(8,128)S(1)}, u32[]{:S(2)}, u32[]{:S(2)}) collective-permute-start(f32[16,24,256]{2,1,0:T(8,128)S(1)} %get-tuple-element.35), channel_id=1, source_target_pairs={{0,1},{1,0},{2,3},{3,2},{4,5},{5,4},{6,7},{7,6},{8,9},{9,8},{10,11... | collective-permute-start | bytes 1179656 | tf_op jit(solution)/shard_map/ppermute | solution.py:415
  65.2 24.4 %all-to-all-start.2 = ((f32[16,24,256]{2,1,0:T(8,128)}), f32[16,24,256]{2,1,0:T(8,128)S(1)}, u32[]{:S(2)}, u32[]{:S(2)}) async-start(f32[16,24,256]{2,1,0:T(8,128)} %shard_map.90), calls=%async_computation.2 | async-start | bytes 786432 | tf_op jit(solution)/shard_map/all_to_all | solution.py:425
